TPU v7x, 32 devices: a whole 2x2x4 slice. The times are simulated.
32 devices in a mesh: depth: 2 (over x), gx: 8 (over z, y), gy: 2 (over core).
Axes of the slice: x: 2, y: 2, z: 4, core: 2. Of those that a mesh axis runs over, the one named last changes fastest.
Arguments:
- operator: bfloat16 [2, 8, 2, 1536, 1536], P('depth', 'gx', 'gy')
- sources: bfloat16 [2, 8, 2, 768, 1024], P('depth', 'gx', 'gy'), may hold values from -6 to 6
Outputs:
- solution: bfloat16 [2, 8, 2, 768, 1024], P('depth', 'gx', 'gy')
All inputs are finite; a program needn't handle non-finite values.
Results may differ from a plain program's by a relative error of at most 0.017.
Values may be sent and summed in bfloat16 or wider, within the bound.
No kernel may reach another device: no remote copies, remote signals or barrier semaphores. Data moves between devices by JAX's collectives and lax.ppermute only.
A program may use at most 64 MiB of HBM per device.

v0:
```python
import jax
import jax.numpy as jnp
from jax import lax
from jax.sharding import PartitionSpec as P

BATCHES = 4


def shifted(block, axis, distance):
    devices = range(lax.axis_size(axis))
    route = [(i - distance, i) for i in devices if i - distance in devices]
    return lax.ppermute(block, axis, route)


def shards(operator, sources):
    local_op = operator[0, 0, 0]
    local_src = sources[0, 0, 0]
    inner = local_src.shape[0]
    trace = (local_op.shape[0] - inner) // 3
    columns = local_src.shape[1]
    pieces = BATCHES
    width = columns // pieces
    level = lax.axis_index("depth") + lax.axis_index("gx") + lax.axis_index("gy")
    ticks = lax.axis_size("depth") + lax.axis_size("gx") + lax.axis_size("gy") - 3 + pieces
    op_trace = local_op[:, : 3 * trace]
    op_source = local_op[:, 3 * trace :]

    def source_part(start):
        block = lax.dynamic_slice_in_dim(local_src, start, width, 1)
        return jnp.dot(op_source, block, preferred_element_type=jnp.float32)

    def tick(step, carry):
        x_in, y_in, z_in, solved = carry
        piece = step - level
        active = jnp.logical_and(piece >= 0, piece < pieces)
        start = jnp.clip(piece, 0, pieces - 1) * width

        def work(state):
            incoming = jnp.concatenate([x_in, y_in, z_in], axis=0)
            total = jnp.dot(op_trace, incoming, preferred_element_type=jnp.float32) + source_part(
                start
            )
            result = total.astype(jnp.bfloat16)
            updated = lax.dynamic_update_slice_in_dim(state, result[3 * trace :], start, 1)
            return (result[: 3 * trace], updated)

        def resting(state):
            return (jnp.zeros((3 * trace, width), jnp.bfloat16), state)

        outgoing, solved = lax.cond(active, work, resting, solved)
        x_next = shifted(outgoing[:trace], "gx", 1)
        y_next = shifted(outgoing[trace : 2 * trace], "gy", 1)
        z_next = shifted(outgoing[2 * trace :], "depth", 1)
        return (x_next, y_next, z_next, solved)

    empty = jnp.zeros((trace, width), jnp.bfloat16)
    start_state = (empty, empty, empty, jnp.zeros((inner, columns), jnp.bfloat16))
    final_state = lax.fori_loop(0, ticks, tick, start_state)
    return final_state[3][None, None, None]


def solution(mesh):
    in_specs = (P("depth", "gx", "gy", None, None), P("depth", "gx", "gy", None, None))
    out_specs = P("depth", "gx", "gy", None, None)
    return jax.shard_map(shards, mesh=mesh, in_specs=in_specs, out_specs=out_specs, check_vma=False)
```

profile of v0, /device:TPU:0, one launch (start us, length us, event | category | flops | bytes accessed | tf_op | source)
XLA Modules:
  0.0 172.2 jit_solution(8532766777164055270)
XLA Ops:
  0.0 4.1 %fusion.12 = (bf16[1536,768]{1,0:T(8,128)(2,1)}, bf16[1536,768]{1,0:T(8,128)(2,1)S(1)}) fusion(bf16[1536,1536]{1,0:T(8,128)(2,1)} %bitcast.7), kind=kLoop, calls=%fused_computation.14 | loop fusion | bytes 9437184 | tf_op jit(solution)/shard_map/slice | solution.py:26
  4.1 1.2 broadcast_in_dim.10
  5.4 164.2 %while.22 = (s32[]{:T(128)}, bf16[256,256]{0,1:T(8,128)(2,1)S(1)}, bf16[256,256]{0,1:T(8,128)(2,1)S(1)}, bf16[256,256]{0,1:T(8,128)(2,1)S(1)}, bf16[768,1024]{0,...) while((s32[]{:T(128)}, bf16[256,256]{0,1:T(8,128)(2,1)S(1)}, ...), condition=%wide.region_3.4_spmd, body=%wide.region_0.3_spmd.sunk | while | flops 1209925632 | bytes 23593420 | solution.py:58
  5.4 4.6 %conditional.2 = (bf16[768,256]{0,1:T(8,128)(2,1)S(1)}, bf16[768,1024]{0,1:T(8,128)(2,1)}) conditional(s32[]{:T(128)} %convert_element_type.18, bf16[768,1024]{0,1:T(8,128)(2,1)} %get-tuple-element.331, (bf16[256,256]{0,1:T(8,128)(2,1)S(1)}, bf16[256,256]{0,1:T(8,128)(2,1)S(1)}, bf16[256,256]{0,1:T(8,128)(2,1)S(1)}, bf16[1536,768]{1,0:T(8,128)(2,1)S(1)}, ...), branch_computations={%region_1.1_spmd, %region_2.2_spmd} | conditional | flops 1209925632 | bytes 21233786 | solution.py:50
  7.4 1.8 %fusion.1 = bf16[1536,256]{0,1:T(8,128)(2,1)S(1)} fusion(f32[256,1536]{1,0:T(8,128)S(1)} %fusion.2, bf16[1536,768]{1,0:T(8,128)(2,1)S(1)} %copy-done, bf16[768,1024]{1,0:T(8,128)(2,1)} %get-tuple-element.195, s32[]{:T(128)S(6)} %select_n.4), kind=kOutput, calls=%fused_computation.2 | convolution fusion | flops 604766208 | bytes 5111812 | tf_op jit(solution)/shard_map/while/body/eval_jaxpr/cond/branch_1_fun/dot_general | solution.py:30
  10.1 1.3 collective-permute-start
  11.4 1.3 collective-permute-start.1
  12.7 2.6 %collective-permute-start.2 = (bf16[256,256]{0,1:T(8,128)(2,1)S(1)}, bf16[256,256]{0,1:T(8,128)(2,1)S(1)}, u32[]{:S(2)}, u32[]{:S(2)}) collective-permute-start(bf16[256,256]{0,1:T(8,128)(2,1)S(1)} %get-tuple-element.309), channel_id=1, source_target_pairs={{0,16},{1,17},{2,18},{3,19},{4,20},{5,21},{6,22},{7,23},{8,24},{9,... | collective-permute-start | bytes 393224 | tf_op jit(solution)/shard_map/while/body/eval_jaxpr/ppermute | solution.py:12
  15.3 2.5 %collective-permute-done.2 = bf16[256,256]{0,1:T(8,128)(2,1)S(1)} collective-permute-done((bf16[256,256]{0,1:T(8,128)(2,1)S(1)}, bf16[256,256]{0,1:T(8,128)(2,1)S(1)}, u32[]{:S(2)}, u32[]{:S(2)}) %collective-permute-start.2) | collective-permute-done | bytes 131104 | tf_op jit(solution)/shard_map/while/body/eval_jaxpr/ppermute | solution.py:12
  17.8 4.6 %conditional.2 = (bf16[768,256]{0,1:T(8,128)(2,1)S(1)}, bf16[768,1024]{0,1:T(8,128)(2,1)}) conditional(s32[]{:T(128)} %convert_element_type.18, bf16[768,1024]{0,1:T(8,128)(2,1)} %get-tuple-element.331, (bf16[256,256]{0,1:T(8,128)(2,1)S(1)}, bf16[256,256]{0,1:T(8,128)(2,1)S(1)}, bf16[256,256]{0,1:T(8,128)(2,1)S(1)}, bf16[1536,768]{1,0:T(8,128)(2,1)S(1)}, ...), branch_computations={%region_1.1_spmd, %region_2.2_spmd} | conditional | flops 1209925632 | bytes 21233786 | solution.py:50
  19.8 1.8 %fusion.1 = bf16[1536,256]{0,1:T(8,128)(2,1)S(1)} fusion(f32[256,1536]{1,0:T(8,128)S(1)} %fusion.2, bf16[1536,768]{1,0:T(8,128)(2,1)S(1)} %copy-done, bf16[768,1024]{1,0:T(8,128)(2,1)} %get-tuple-element.195, s32[]{:T(128)S(6)} %select_n.4), kind=kOutput, calls=%fused_computation.2 | convolution fusion | flops 604766208 | bytes 5111812 | tf_op jit(solution)/shard_map/while/body/eval_jaxpr/cond/branch_1_fun/dot_general | solution.py:30
  22.4 3.4 %collective-permute-start = (bf16[256,256]{0,1:T(8,128)(2,1)S(1)}, bf16[256,256]{0,1:T(8,128)(2,1)S(1)}, u32[]{:S(2)}, u32[]{:S(2)}) collective-permute-start(bf16[256,256]{0,1:T(8,128)(2,1)S(1)} %get-tuple-element.307), channel_id=1, source_target_pairs={{0,2},{2,4},{4,6},{6,8},{8,10},{10,12},{12,14},{1,3},{3,5},{5,7},{... | collective-permute-start | bytes 393224 | tf_op jit(solution)/shard_map/while/body/eval_jaxpr/ppermute | solution.py:12
  25.9 1.3 collective-permute-start.1
  27.2 2.2 %collective-permute-start.2 = (bf16[256,256]{0,1:T(8,128)(2,1)S(1)}, bf16[256,256]{0,1:T(8,128)(2,1)S(1)}, u32[]{:S(2)}, u32[]{:S(2)}) collective-permute-start(bf16[256,256]{0,1:T(8,128)(2,1)S(1)} %get-tuple-element.309), channel_id=1, source_target_pairs={{0,16},{1,17},{2,18},{3,19},{4,20},{5,21},{6,22},{7,23},{8,24},{9,... | collective-permute-start | bytes 393224 | tf_op jit(solution)/shard_map/while/body/eval_jaxpr/ppermute | solution.py:12
  29.4 2.5 %collective-permute-done.2 = bf16[256,256]{0,1:T(8,128)(2,1)S(1)} collective-permute-done((bf16[256,256]{0,1:T(8,128)(2,1)S(1)}, bf16[256,256]{0,1:T(8,128)(2,1)S(1)}, u32[]{:S(2)}, u32[]{:S(2)}) %collective-permute-start.2) | collective-permute-done | bytes 131104 | tf_op jit(solution)/shard_map/while/body/eval_jaxpr/ppermute | solution.py:12
  31.9 4.6 %conditional.2 = (bf16[768,256]{0,1:T(8,128)(2,1)S(1)}, bf16[768,1024]{0,1:T(8,128)(2,1)}) conditional(s32[]{:T(128)} %convert_element_type.18, bf16[768,1024]{0,1:T(8,128)(2,1)} %get-tuple-element.331, (bf16[256,256]{0,1:T(8,128)(2,1)S(1)}, bf16[256,256]{0,1:T(8,128)(2,1)S(1)}, bf16[256,256]{0,1:T(8,128)(2,1)S(1)}, bf16[1536,768]{1,0:T(8,128)(2,1)S(1)}, ...), branch_computations={%region_1.1_spmd, %region_2.2_spmd} | conditional | flops 1209925632 | bytes 21233786 | solution.py:50
  33.9 1.8 %fusion.1 = bf16[1536,256]{0,1:T(8,128)(2,1)S(1)} fusion(f32[256,1536]{1,0:T(8,128)S(1)} %fusion.2, bf16[1536,768]{1,0:T(8,128)(2,1)S(1)} %copy-done, bf16[768,1024]{1,0:T(8,128)(2,1)} %get-tuple-element.195, s32[]{:T(128)S(6)} %select_n.4), kind=kOutput, calls=%fused_computation.2 | convolution fusion | flops 604766208 | bytes 5111812 | tf_op jit(solution)/shard_map/while/body/eval_jaxpr/cond/branch_1_fun/dot_general | solution.py:30
  36.6 1.3 collective-permute-start
  37.9 1.3 collective-permute-start.1
  39.2 4.4 %collective-permute-start.2 = (bf16[256,256]{0,1:T(8,128)(2,1)S(1)}, bf16[256,256]{0,1:T(8,128)(2,1)S(1)}, u32[]{:S(2)}, u32[]{:S(2)}) collective-permute-start(bf16[256,256]{0,1:T(8,128)(2,1)S(1)} %get-tuple-element.309), channel_id=1, source_target_pairs={{0,16},{1,17},{2,18},{3,19},{4,20},{5,21},{6,22},{7,23},{8,24},{9,... | collective-permute-start | bytes 393224 | tf_op jit(solution)/shard_map/while/body/eval_jaxpr/ppermute | solution.py:12
  43.6 2.5 %collective-permute-done.2 = bf16[256,256]{0,1:T(8,128)(2,1)S(1)} collective-permute-done((bf16[256,256]{0,1:T(8,128)(2,1)S(1)}, bf16[256,256]{0,1:T(8,128)(2,1)S(1)}, u32[]{:S(2)}, u32[]{:S(2)}) %collective-permute-start.2) | collective-permute-done | bytes 131104 | tf_op jit(solution)/shard_map/while/body/eval_jaxpr/ppermute | solution.py:12
  46.1 4.6 %conditional.2 = (bf16[768,256]{0,1:T(8,128)(2,1)S(1)}, bf16[768,1024]{0,1:T(8,128)(2,1)}) conditional(s32[]{:T(128)} %convert_element_type.18, bf16[768,1024]{0,1:T(8,128)(2,1)} %get-tuple-element.331, (bf16[256,256]{0,1:T(8,128)(2,1)S(1)}, bf16[256,256]{0,1:T(8,128)(2,1)S(1)}, bf16[256,256]{0,1:T(8,128)(2,1)S(1)}, bf16[1536,768]{1,0:T(8,128)(2,1)S(1)}, ...), branch_computations={%region_1.1_spmd, %region_2.2_spmd} | conditional | flops 1209925632 | bytes 21233786 | solution.py:50
  48.0 1.8 %fusion.1 = bf16[1536,256]{0,1:T(8,128)(2,1)S(1)} fusion(f32[256,1536]{1,0:T(8,128)S(1)} %fusion.2, bf16[1536,768]{1,0:T(8,128)(2,1)S(1)} %copy-done, bf16[768,1024]{1,0:T(8,128)(2,1)} %get-tuple-element.195, s32[]{:T(128)S(6)} %select_n.4), kind=kOutput, calls=%fused_computation.2 | convolution fusion | flops 604766208 | bytes 5111812 | tf_op jit(solution)/shard_map/while/body/eval_jaxpr/cond/branch_1_fun/dot_general | solution.py:30
  50.7 1.6 collective-permute-start
  52.3 1.3 collective-permute-start.1
  53.6 4.4 %collective-permute-start.2 = (bf16[256,256]{0,1:T(8,128)(2,1)S(1)}, bf16[256,256]{0,1:T(8,128)(2,1)S(1)}, u32[]{:S(2)}, u32[]{:S(2)}) collective-permute-start(bf16[256,256]{0,1:T(8,128)(2,1)S(1)} %get-tuple-element.309), channel_id=1, source_target_pairs={{0,16},{1,17},{2,18},{3,19},{4,20},{5,21},{6,22},{7,23},{8,24},{9,... | collective-permute-start | bytes 393224 | tf_op jit(solution)/shard_map/while/body/eval_jaxpr/ppermute | solution.py:12
  58.1 2.5 %collective-permute-done.2 = bf16[256,256]{0,1:T(8,128)(2,1)S(1)} collective-permute-done((bf16[256,256]{0,1:T(8,128)(2,1)S(1)}, bf16[256,256]{0,1:T(8,128)(2,1)S(1)}, u32[]{:S(2)}, u32[]{:S(2)}) %collective-permute-start.2) | collective-permute-done | bytes 131104 | tf_op jit(solution)/shard_map/while/body/eval_jaxpr/ppermute | solution.py:12
  60.6 6.5 %collective-permute-start = (bf16[256,256]{0,1:T(8,128)(2,1)S(1)}, bf16[256,256]{0,1:T(8,128)(2,1)S(1)}, u32[]{:S(2)}, u32[]{:S(2)}) collective-permute-start(bf16[256,256]{0,1:T(8,128)(2,1)S(1)} %get-tuple-element.307), channel_id=1, source_target_pairs={{0,2},{2,4},{4,6},{6,8},{8,10},{10,12},{12,14},{1,3},{3,5},{5,7},{... | collective-permute-start | bytes 393224 | tf_op jit(solution)/shard_map/while/body/eval_jaxpr/ppermute | solution.py:12
  67.1 1.3 collective-permute-start.1
  68.4 4.4 %collective-permute-start.2 = (bf16[256,256]{0,1:T(8,128)(2,1)S(1)}, bf16[256,256]{0,1:T(8,128)(2,1)S(1)}, u32[]{:S(2)}, u32[]{:S(2)}) collective-permute-start(bf16[256,256]{0,1:T(8,128)(2,1)S(1)} %get-tuple-element.309), channel_id=1, source_target_pairs={{0,16},{1,17},{2,18},{3,19},{4,20},{5,21},{6,22},{7,23},{8,24},{9,... | collective-permute-start | bytes 393224 | tf_op jit(solution)/shard_map/while/body/eval_jaxpr/ppermute | solution.py:12
  72.8 2.5 %collective-permute-done.2 = bf16[256,256]{0,1:T(8,128)(2,1)S(1)} collective-permute-done((bf16[256,256]{0,1:T(8,128)(2,1)S(1)}, bf16[256,256]{0,1:T(8,128)(2,1)S(1)}, u32[]{:S(2)}, u32[]{:S(2)}) %collective-permute-start.2) | collective-permute-done | bytes 131104 | tf_op jit(solution)/shard_map/while/body/eval_jaxpr/ppermute | solution.py:12
  75.4 1.9 %collective-permute-start = (bf16[256,256]{0,1:T(8,128)(2,1)S(1)}, bf16[256,256]{0,1:T(8,128)(2,1)S(1)}, u32[]{:S(2)}, u32[]{:S(2)}) collective-permute-start(bf16[256,256]{0,1:T(8,128)(2,1)S(1)} %get-tuple-element.307), channel_id=1, source_target_pairs={{0,2},{2,4},{4,6},{6,8},{8,10},{10,12},{12,14},{1,3},{3,5},{5,7},{... | collective-permute-start | bytes 393224 | tf_op jit(solution)/shard_map/while/body/eval_jaxpr/ppermute | solution.py:12
  77.3 1.3 collective-permute-start.1
  78.6 8.9 %collective-permute-start.2 = (bf16[256,256]{0,1:T(8,128)(2,1)S(1)}, bf16[256,256]{0,1:T(8,128)(2,1)S(1)}, u32[]{:S(2)}, u32[]{:S(2)}) collective-permute-start(bf16[256,256]{0,1:T(8,128)(2,1)S(1)} %get-tuple-element.309), channel_id=1, source_target_pairs={{0,16},{1,17},{2,18},{3,19},{4,20},{5,21},{6,22},{7,23},{8,24},{9,... | collective-permute-start | bytes 393224 | tf_op jit(solution)/shard_map/while/body/eval_jaxpr/ppermute | solution.py:12
  87.6 2.5 %collective-permute-done.2 = bf16[256,256]{0,1:T(8,128)(2,1)S(1)} collective-permute-done((bf16[256,256]{0,1:T(8,128)(2,1)S(1)}, bf16[256,256]{0,1:T(8,128)(2,1)S(1)}, u32[]{:S(2)}, u32[]{:S(2)}) %collective-permute-start.2) | collective-permute-done | bytes 131104 | tf_op jit(solution)/shard_map/while/body/eval_jaxpr/ppermute | solution.py:12
  90.1 1.9 %collective-permute-start = (bf16[256,256]{0,1:T(8,128)(2,1)S(1)}, bf16[256,256]{0,1:T(8,128)(2,1)S(1)}, u32[]{:S(2)}, u32[]{:S(2)}) collective-permute-start(bf16[256,256]{0,1:T(8,128)(2,1)S(1)} %get-tuple-element.307), channel_id=1, source_target_pairs={{0,2},{2,4},{4,6},{6,8},{8,10},{10,12},{12,14},{1,3},{3,5},{5,7},{... | collective-permute-start | bytes 393224 | tf_op jit(solution)/shard_map/while/body/eval_jaxpr/ppermute | solution.py:12
  92.1 1.3 collective-permute-start.1
  93.4 4.4 %collective-permute-start.2 = (bf16[256,256]{0,1:T(8,128)(2,1)S(1)}, bf16[256,256]{0,1:T(8,128)(2,1)S(1)}, u32[]{:S(2)}, u32[]{:S(2)}) collective-permute-start(bf16[256,256]{0,1:T(8,128)(2,1)S(1)} %get-tuple-element.309), channel_id=1, source_target_pairs={{0,16},{1,17},{2,18},{3,19},{4,20},{5,21},{6,22},{7,23},{8,24},{9,... | collective-permute-start | bytes 393224 | tf_op jit(solution)/shard_map/while/body/eval_jaxpr/ppermute | solution.py:12
  97.7 2.5 %collective-permute-done.2 = bf16[256,256]{0,1:T(8,128)(2,1)S(1)} collective-permute-done((bf16[256,256]{0,1:T(8,128)(2,1)S(1)}, bf16[256,256]{0,1:T(8,128)(2,1)S(1)}, u32[]{:S(2)}, u32[]{:S(2)}) %collective-permute-start.2) | collective-permute-done | bytes 131104 | tf_op jit(solution)/shard_map/while/body/eval_jaxpr/ppermute | solution.py:12
  100.3 4.9 %collective-permute-start = (bf16[256,256]{0,1:T(8,128)(2,1)S(1)}, bf16[256,256]{0,1:T(8,128)(2,1)S(1)}, u32[]{:S(2)}, u32[]{:S(2)}) collective-permute-start(bf16[256,256]{0,1:T(8,128)(2,1)S(1)} %get-tuple-element.307), channel_id=1, source_target_pairs={{0,2},{2,4},{4,6},{6,8},{8,10},{10,12},{12,14},{1,3},{3,5},{5,7},{... | collective-permute-start | bytes 393224 | tf_op jit(solution)/shard_map/while/body/eval_jaxpr/ppermute | solution.py:12
  105.2 1.3 collective-permute-start.1
  106.6 4.4 %collective-permute-start.2 = (bf16[256,256]{0,1:T(8,128)(2,1)S(1)}, bf16[256,256]{0,1:T(8,128)(2,1)S(1)}, u32[]{:S(2)}, u32[]{:S(2)}) collective-permute-start(bf16[256,256]{0,1:T(8,128)(2,1)S(1)} %get-tuple-element.309), channel_id=1, source_target_pairs={{0,16},{1,17},{2,18},{3,19},{4,20},{5,21},{6,22},{7,23},{8,24},{9,... | collective-permute-start | bytes 393224 | tf_op jit(solution)/shard_map/while/body/eval_jaxpr/ppermute | solution.py:12
  110.9 2.5 %collective-permute-done.2 = bf16[256,256]{0,1:T(8,128)(2,1)S(1)} collective-permute-done((bf16[256,256]{0,1:T(8,128)(2,1)S(1)}, bf16[256,256]{0,1:T(8,128)(2,1)S(1)}, u32[]{:S(2)}, u32[]{:S(2)}) %collective-permute-start.2) | collective-permute-done | bytes 131104 | tf_op jit(solution)/shard_map/while/body/eval_jaxpr/ppermute | solution.py:12
  113.5 1.9 %collective-permute-start = (bf16[256,256]{0,1:T(8,128)(2,1)S(1)}, bf16[256,256]{0,1:T(8,128)(2,1)S(1)}, u32[]{:S(2)}, u32[]{:S(2)}) collective-permute-start(bf16[256,256]{0,1:T(8,128)(2,1)S(1)} %get-tuple-element.307), channel_id=1, source_target_pairs={{0,2},{2,4},{4,6},{6,8},{8,10},{10,12},{12,14},{1,3},{3,5},{5,7},{... | collective-permute-start | bytes 393224 | tf_op jit(solution)/shard_map/while/body/eval_jaxpr/ppermute | solution.py:12
  115.4 1.3 collective-permute-start.1
  116.7 4.4 %collective-permute-start.2 = (bf16[256,256]{0,1:T(8,128)(2,1)S(1)}, bf16[256,256]{0,1:T(8,128)(2,1)S(1)}, u32[]{:S(2)}, u32[]{:S(2)}) collective-permute-start(bf16[256,256]{0,1:T(8,128)(2,1)S(1)} %get-tuple-element.309), channel_id=1, source_target_pairs={{0,16},{1,17},{2,18},{3,19},{4,20},{5,21},{6,22},{7,23},{8,24},{9,... | collective-permute-start | bytes 393224 | tf_op jit(solution)/shard_map/while/body/eval_jaxpr/ppermute | solution.py:12
  121.1 2.5 %collective-permute-done.2 = bf16[256,256]{0,1:T(8,128)(2,1)S(1)} collective-permute-done((bf16[256,256]{0,1:T(8,128)(2,1)S(1)}, bf16[256,256]{0,1:T(8,128)(2,1)S(1)}, u32[]{:S(2)}, u32[]{:S(2)}) %collective-permute-start.2) | collective-permute-done | bytes 131104 | tf_op jit(solution)/shard_map/while/body/eval_jaxpr/ppermute | solution.py:12
  123.7 4.9 %collective-permute-start = (bf16[256,256]{0,1:T(8,128)(2,1)S(1)}, bf16[256,256]{0,1:T(8,128)(2,1)S(1)}, u32[]{:S(2)}, u32[]{:S(2)}) collective-permute-start(bf16[256,256]{0,1:T(8,128)(2,1)S(1)} %get-tuple-element.307), channel_id=1, source_target_pairs={{0,2},{2,4},{4,6},{6,8},{8,10},{10,12},{12,14},{1,3},{3,5},{5,7},{... | collective-permute-start | bytes 393224 | tf_op jit(solution)/shard_map/while/body/eval_jaxpr/ppermute | solution.py:12
  128.6 1.3 collective-permute-start.1
  129.9 4.4 %collective-permute-start.2 = (bf16[256,256]{0,1:T(8,128)(2,1)S(1)}, bf16[256,256]{0,1:T(8,128)(2,1)S(1)}, u32[]{:S(2)}, u32[]{:S(2)}) collective-permute-start(bf16[256,256]{0,1:T(8,128)(2,1)S(1)} %get-tuple-element.309), channel_id=1, source_target_pairs={{0,16},{1,17},{2,18},{3,19},{4,20},{5,21},{6,22},{7,23},{8,24},{9,... | collective-permute-start | bytes 393224 | tf_op jit(solution)/shard_map/while/body/eval_jaxpr/ppermute | solution.py:12
  134.3 2.5 %collective-permute-done.2 = bf16[256,256]{0,1:T(8,128)(2,1)S(1)} collective-permute-done((bf16[256,256]{0,1:T(8,128)(2,1)S(1)}, bf16[256,256]{0,1:T(8,128)(2,1)S(1)}, u32[]{:S(2)}, u32[]{:S(2)}) %collective-permute-start.2) | collective-permute-done | bytes 131104 | tf_op jit(solution)/shard_map/while/body/eval_jaxpr/ppermute | solution.py:12
  136.9 1.9 %collective-permute-start = (bf16[256,256]{0,1:T(8,128)(2,1)S(1)}, bf16[256,256]{0,1:T(8,128)(2,1)S(1)}, u32[]{:S(2)}, u32[]{:S(2)}) collective-permute-start(bf16[256,256]{0,1:T(8,128)(2,1)S(1)} %get-tuple-element.307), channel_id=1, source_target_pairs={{0,2},{2,4},{4,6},{6,8},{8,10},{10,12},{12,14},{1,3},{3,5},{5,7},{... | collective-permute-start | bytes 393224 | tf_op jit(solution)/shard_map/while/body/eval_jaxpr/ppermute | solution.py:12
  138.8 1.3 collective-permute-start.1
  140.1 4.4 %collective-permute-start.2 = (bf16[256,256]{0,1:T(8,128)(2,1)S(1)}, bf16[256,256]{0,1:T(8,128)(2,1)S(1)}, u32[]{:S(2)}, u32[]{:S(2)}) collective-permute-start(bf16[256,256]{0,1:T(8,128)(2,1)S(1)} %get-tuple-element.309), channel_id=1, source_target_pairs={{0,16},{1,17},{2,18},{3,19},{4,20},{5,21},{6,22},{7,23},{8,24},{9,... | collective-permute-start | bytes 393224 | tf_op jit(solution)/shard_map/while/body/eval_jaxpr/ppermute | solution.py:12
  144.5 2.5 %collective-permute-done.2 = bf16[256,256]{0,1:T(8,128)(2,1)S(1)} collective-permute-done((bf16[256,256]{0,1:T(8,128)(2,1)S(1)}, bf16[256,256]{0,1:T(8,128)(2,1)S(1)}, u32[]{:S(2)}, u32[]{:S(2)}) %collective-permute-start.2) | collective-permute-done | bytes 131104 | tf_op jit(solution)/shard_map/while/body/eval_jaxpr/ppermute | solution.py:12
  147.1 4.2 %collective-permute-start = (bf16[256,256]{0,1:T(8,128)(2,1)S(1)}, bf16[256,256]{0,1:T(8,128)(2,1)S(1)}, u32[]{:S(2)}, u32[]{:S(2)}) collective-permute-start(bf16[256,256]{0,1:T(8,128)(2,1)S(1)} %get-tuple-element.307), channel_id=1, source_target_pairs={{0,2},{2,4},{4,6},{6,8},{8,10},{10,12},{12,14},{1,3},{3,5},{5,7},{... | collective-permute-start | bytes 393224 | tf_op jit(solution)/shard_map/while/body/eval_jaxpr/ppermute | solution.py:12
  151.2 1.3 collective-permute-start.1
  152.6 4.4 %collective-permute-start.2 = (bf16[256,256]{0,1:T(8,128)(2,1)S(1)}, bf16[256,256]{0,1:T(8,128)(2,1)S(1)}, u32[]{:S(2)}, u32[]{:S(2)}) collective-permute-start(bf16[256,256]{0,1:T(8,128)(2,1)S(1)} %get-tuple-element.309), channel_id=1, source_target_pairs={{0,16},{1,17},{2,18},{3,19},{4,20},{5,21},{6,22},{7,23},{8,24},{9,... | collective-permute-start | bytes 393224 | tf_op jit(solution)/shard_map/while/body/eval_jaxpr/ppermute | solution.py:12
  156.9 2.5 %collective-permute-done.2 = bf16[256,256]{0,1:T(8,128)(2,1)S(1)} collective-permute-done((bf16[256,256]{0,1:T(8,128)(2,1)S(1)}, bf16[256,256]{0,1:T(8,128)(2,1)S(1)}, u32[]{:S(2)}, u32[]{:S(2)}) %collective-permute-start.2) | collective-permute-done | bytes 131104 | tf_op jit(solution)/shard_map/while/body/eval_jaxpr/ppermute | solution.py:12
  159.5 1.9 %collective-permute-start = (bf16[256,256]{0,1:T(8,128)(2,1)S(1)}, bf16[256,256]{0,1:T(8,128)(2,1)S(1)}, u32[]{:S(2)}, u32[]{:S(2)}) collective-permute-start(bf16[256,256]{0,1:T(8,128)(2,1)S(1)} %get-tuple-element.307), channel_id=1, source_target_pairs={{0,2},{2,4},{4,6},{6,8},{8,10},{10,12},{12,14},{1,3},{3,5},{5,7},{... | collective-permute-start | bytes 393224 | tf_op jit(solution)/shard_map/while/body/eval_jaxpr/ppermute | solution.py:12
  161.4 1.3 collective-permute-start.1
  162.7 4.4 %collective-permute-start.2 = (bf16[256,256]{0,1:T(8,128)(2,1)S(1)}, bf16[256,256]{0,1:T(8,128)(2,1)S(1)}, u32[]{:S(2)}, u32[]{:S(2)}) collective-permute-start(bf16[256,256]{0,1:T(8,128)(2,1)S(1)} %get-tuple-element.309), channel_id=1, source_target_pairs={{0,16},{1,17},{2,18},{3,19},{4,20},{5,21},{6,22},{7,23},{8,24},{9,... | collective-permute-start | bytes 393224 | tf_op jit(solution)/shard_map/while/body/eval_jaxpr/ppermute | solution.py:12
  167.1 2.5 %collective-permute-done.2 = bf16[256,256]{0,1:T(8,128)(2,1)S(1)} collective-permute-done((bf16[256,256]{0,1:T(8,128)(2,1)S(1)}, bf16[256,256]{0,1:T(8,128)(2,1)S(1)}, u32[]{:S(2)}, u32[]{:S(2)}) %collective-permute-start.2) | collective-permute-done | bytes 131104 | tf_op jit(solution)/shard_map/while/body/eval_jaxpr/ppermute | solution.py:12
  169.6 2.6 %copy.6 = bf16[768,1024]{1,0:T(8,128)(2,1)} copy(bf16[768,1024]{0,1:T(8,128)(2,1)} %get-tuple-element.212) | data formatting | bytes 3145728 | tf_op jit(solution)/shard_map/while | solution.py:58
  (88 shorter events, 12.1 us)
Async XLA Ops:
  5.7 1.7 copy-start
  10.1 5.2 %collective-permute-start = (bf16[256,256]{0,1:T(8,128)(2,1)S(1)}, bf16[256,256]{0,1:T(8,128)(2,1)S(1)}, u32[]{:S(2)}, u32[]{:S(2)}) collective-permute-start(bf16[256,256]{0,1:T(8,128)(2,1)S(1)} %get-tuple-element.307), channel_id=1, source_target_pairs={{0,2},{2,4},{4,6},{6,8},{8,10},{10,12},{12,14},{1,3},{3,5},{5,7},{... | collective-permute-start | bytes 393224 | tf_op jit(solution)/shard_map/while/body/eval_jaxpr/ppermute | solution.py:12
  11.4 3.9 %collective-permute-start.1 = (bf16[256,256]{0,1:T(8,128)(2,1)S(1)}, bf16[256,256]{0,1:T(8,128)(2,1)S(1)}, u32[]{:S(2)}, u32[]{:S(2)}) collective-permute-start(bf16[256,256]{0,1:T(8,128)(2,1)S(1)} %get-tuple-element.308), channel_id=1, source_target_pairs={{0,1},{2,3},{4,5},{6,7},{8,9},{10,11},{12,13},{14,15},{16,17},{18,... | collective-permute-start | bytes 393224 | tf_op jit(solution)/shard_map/while/body/eval_jaxpr/ppermute | solution.py:12
  12.7 5.1 %collective-permute-start.2 = (bf16[256,256]{0,1:T(8,128)(2,1)S(1)}, bf16[256,256]{0,1:T(8,128)(2,1)S(1)}, u32[]{:S(2)}, u32[]{:S(2)}) collective-permute-start(bf16[256,256]{0,1:T(8,128)(2,1)S(1)} %get-tuple-element.309), channel_id=1, source_target_pairs={{0,16},{1,17},{2,18},{3,19},{4,20},{5,21},{6,22},{7,23},{8,24},{9,... | collective-permute-start | bytes 393224 | tf_op jit(solution)/shard_map/while/body/eval_jaxpr/ppermute | solution.py:12
  18.1 1.7 copy-start
  22.4 7.0 %collective-permute-start = (bf16[256,256]{0,1:T(8,128)(2,1)S(1)}, bf16[256,256]{0,1:T(8,128)(2,1)S(1)}, u32[]{:S(2)}, u32[]{:S(2)}) collective-permute-start(bf16[256,256]{0,1:T(8,128)(2,1)S(1)} %get-tuple-element.307), channel_id=1, source_target_pairs={{0,2},{2,4},{4,6},{6,8},{8,10},{10,12},{12,14},{1,3},{3,5},{5,7},{... | collective-permute-start | bytes 393224 | tf_op jit(solution)/shard_map/while/body/eval_jaxpr/ppermute | solution.py:12
  25.9 3.6 %collective-permute-start.1 = (bf16[256,256]{0,1:T(8,128)(2,1)S(1)}, bf16[256,256]{0,1:T(8,128)(2,1)S(1)}, u32[]{:S(2)}, u32[]{:S(2)}) collective-permute-start(bf16[256,256]{0,1:T(8,128)(2,1)S(1)} %get-tuple-element.308), channel_id=1, source_target_pairs={{0,1},{2,3},{4,5},{6,7},{8,9},{10,11},{12,13},{14,15},{16,17},{18,... | collective-permute-start | bytes 393224 | tf_op jit(solution)/shard_map/while/body/eval_jaxpr/ppermute | solution.py:12
  27.2 4.7 %collective-permute-start.2 = (bf16[256,256]{0,1:T(8,128)(2,1)S(1)}, bf16[256,256]{0,1:T(8,128)(2,1)S(1)}, u32[]{:S(2)}, u32[]{:S(2)}) collective-permute-start(bf16[256,256]{0,1:T(8,128)(2,1)S(1)} %get-tuple-element.309), channel_id=1, source_target_pairs={{0,16},{1,17},{2,18},{3,19},{4,20},{5,21},{6,22},{7,23},{8,24},{9,... | collective-permute-start | bytes 393224 | tf_op jit(solution)/shard_map/while/body/eval_jaxpr/ppermute | solution.py:12
  32.2 1.7 copy-start
  36.6 7.0 %collective-permute-start = (bf16[256,256]{0,1:T(8,128)(2,1)S(1)}, bf16[256,256]{0,1:T(8,128)(2,1)S(1)}, u32[]{:S(2)}, u32[]{:S(2)}) collective-permute-start(bf16[256,256]{0,1:T(8,128)(2,1)S(1)} %get-tuple-element.307), channel_id=1, source_target_pairs={{0,2},{2,4},{4,6},{6,8},{8,10},{10,12},{12,14},{1,3},{3,5},{5,7},{... | collective-permute-start | bytes 393224 | tf_op jit(solution)/shard_map/while/body/eval_jaxpr/ppermute | solution.py:12
  37.9 5.7 %collective-permute-start.1 = (bf16[256,256]{0,1:T(8,128)(2,1)S(1)}, bf16[256,256]{0,1:T(8,128)(2,1)S(1)}, u32[]{:S(2)}, u32[]{:S(2)}) collective-permute-start(bf16[256,256]{0,1:T(8,128)(2,1)S(1)} %get-tuple-element.308), channel_id=1, source_target_pairs={{0,1},{2,3},{4,5},{6,7},{8,9},{10,11},{12,13},{14,15},{16,17},{18,... | collective-permute-start | bytes 393224 | tf_op jit(solution)/shard_map/while/body/eval_jaxpr/ppermute | solution.py:12
  39.2 6.9 %collective-permute-start.2 = (bf16[256,256]{0,1:T(8,128)(2,1)S(1)}, bf16[256,256]{0,1:T(8,128)(2,1)S(1)}, u32[]{:S(2)}, u32[]{:S(2)}) collective-permute-start(bf16[256,256]{0,1:T(8,128)(2,1)S(1)} %get-tuple-element.309), channel_id=1, source_target_pairs={{0,16},{1,17},{2,18},{3,19},{4,20},{5,21},{6,22},{7,23},{8,24},{9,... | collective-permute-start | bytes 393224 | tf_op jit(solution)/shard_map/while/body/eval_jaxpr/ppermute | solution.py:12
  46.4 1.7 copy-start
  50.7 7.3 %collective-permute-start = (bf16[256,256]{0,1:T(8,128)(2,1)S(1)}, bf16[256,256]{0,1:T(8,128)(2,1)S(1)}, u32[]{:S(2)}, u32[]{:S(2)}) collective-permute-start(bf16[256,256]{0,1:T(8,128)(2,1)S(1)} %get-tuple-element.307), channel_id=1, source_target_pairs={{0,2},{2,4},{4,6},{6,8},{8,10},{10,12},{12,14},{1,3},{3,5},{5,7},{... | collective-permute-start | bytes 393224 | tf_op jit(solution)/shard_map/while/body/eval_jaxpr/ppermute | solution.py:12
  52.3 5.7 %collective-permute-start.1 = (bf16[256,256]{0,1:T(8,128)(2,1)S(1)}, bf16[256,256]{0,1:T(8,128)(2,1)S(1)}, u32[]{:S(2)}, u32[]{:S(2)}) collective-permute-start(bf16[256,256]{0,1:T(8,128)(2,1)S(1)} %get-tuple-element.308), channel_id=1, source_target_pairs={{0,1},{2,3},{4,5},{6,7},{8,9},{10,11},{12,13},{14,15},{16,17},{18,... | collective-permute-start | bytes 393224 | tf_op jit(solution)/shard_map/while/body/eval_jaxpr/ppermute | solution.py:12
  53.6 6.9 %collective-permute-start.2 = (bf16[256,256]{0,1:T(8,128)(2,1)S(1)}, bf16[256,256]{0,1:T(8,128)(2,1)S(1)}, u32[]{:S(2)}, u32[]{:S(2)}) collective-permute-start(bf16[256,256]{0,1:T(8,128)(2,1)S(1)} %get-tuple-element.309), channel_id=1, source_target_pairs={{0,16},{1,17},{2,18},{3,19},{4,20},{5,21},{6,22},{7,23},{8,24},{9,... | collective-permute-start | bytes 393224 | tf_op jit(solution)/shard_map/while/body/eval_jaxpr/ppermute | solution.py:12
  60.6 12.2 %collective-permute-start = (bf16[256,256]{0,1:T(8,128)(2,1)S(1)}, bf16[256,256]{0,1:T(8,128)(2,1)S(1)}, u32[]{:S(2)}, u32[]{:S(2)}) collective-permute-start(bf16[256,256]{0,1:T(8,128)(2,1)S(1)} %get-tuple-element.307), channel_id=1, source_target_pairs={{0,2},{2,4},{4,6},{6,8},{8,10},{10,12},{12,14},{1,3},{3,5},{5,7},{... | collective-permute-start | bytes 393224 | tf_op jit(solution)/shard_map/while/body/eval_jaxpr/ppermute | solution.py:12
  67.1 5.7 %collective-permute-start.1 = (bf16[256,256]{0,1:T(8,128)(2,1)S(1)}, bf16[256,256]{0,1:T(8,128)(2,1)S(1)}, u32[]{:S(2)}, u32[]{:S(2)}) collective-permute-start(bf16[256,256]{0,1:T(8,128)(2,1)S(1)} %get-tuple-element.308), channel_id=1, source_target_pairs={{0,1},{2,3},{4,5},{6,7},{8,9},{10,11},{12,13},{14,15},{16,17},{18,... | collective-permute-start | bytes 393224 | tf_op jit(solution)/shard_map/while/body/eval_jaxpr/ppermute | solution.py:12
  68.4 6.9 %collective-permute-start.2 = (bf16[256,256]{0,1:T(8,128)(2,1)S(1)}, bf16[256,256]{0,1:T(8,128)(2,1)S(1)}, u32[]{:S(2)}, u32[]{:S(2)}) collective-permute-start(bf16[256,256]{0,1:T(8,128)(2,1)S(1)} %get-tuple-element.309), channel_id=1, source_target_pairs={{0,16},{1,17},{2,18},{3,19},{4,20},{5,21},{6,22},{7,23},{8,24},{9,... | collective-permute-start | bytes 393224 | tf_op jit(solution)/shard_map/while/body/eval_jaxpr/ppermute | solution.py:12
  75.4 12.2 %collective-permute-start = (bf16[256,256]{0,1:T(8,128)(2,1)S(1)}, bf16[256,256]{0,1:T(8,128)(2,1)S(1)}, u32[]{:S(2)}, u32[]{:S(2)}) collective-permute-start(bf16[256,256]{0,1:T(8,128)(2,1)S(1)} %get-tuple-element.307), channel_id=1, source_target_pairs={{0,2},{2,4},{4,6},{6,8},{8,10},{10,12},{12,14},{1,3},{3,5},{5,7},{... | collective-permute-start | bytes 393224 | tf_op jit(solution)/shard_map/while/body/eval_jaxpr/ppermute | solution.py:12
  77.3 10.3 %collective-permute-start.1 = (bf16[256,256]{0,1:T(8,128)(2,1)S(1)}, bf16[256,256]{0,1:T(8,128)(2,1)S(1)}, u32[]{:S(2)}, u32[]{:S(2)}) collective-permute-start(bf16[256,256]{0,1:T(8,128)(2,1)S(1)} %get-tuple-element.308), channel_id=1, source_target_pairs={{0,1},{2,3},{4,5},{6,7},{8,9},{10,11},{12,13},{14,15},{16,17},{18,... | collective-permute-start | bytes 393224 | tf_op jit(solution)/shard_map/while/body/eval_jaxpr/ppermute | solution.py:12
  78.6 11.4 %collective-permute-start.2 = (bf16[256,256]{0,1:T(8,128)(2,1)S(1)}, bf16[256,256]{0,1:T(8,128)(2,1)S(1)}, u32[]{:S(2)}, u32[]{:S(2)}) collective-permute-start(bf16[256,256]{0,1:T(8,128)(2,1)S(1)} %get-tuple-element.309), channel_id=1, source_target_pairs={{0,16},{1,17},{2,18},{3,19},{4,20},{5,21},{6,22},{7,23},{8,24},{9,... | collective-permute-start | bytes 393224 | tf_op jit(solution)/shard_map/while/body/eval_jaxpr/ppermute | solution.py:12
  90.1 7.6 %collective-permute-start = (bf16[256,256]{0,1:T(8,128)(2,1)S(1)}, bf16[256,256]{0,1:T(8,128)(2,1)S(1)}, u32[]{:S(2)}, u32[]{:S(2)}) collective-permute-start(bf16[256,256]{0,1:T(8,128)(2,1)S(1)} %get-tuple-element.307), channel_id=1, source_target_pairs={{0,2},{2,4},{4,6},{6,8},{8,10},{10,12},{12,14},{1,3},{3,5},{5,7},{... | collective-permute-start | bytes 393224 | tf_op jit(solution)/shard_map/while/body/eval_jaxpr/ppermute | solution.py:12
  92.1 5.7 %collective-permute-start.1 = (bf16[256,256]{0,1:T(8,128)(2,1)S(1)}, bf16[256,256]{0,1:T(8,128)(2,1)S(1)}, u32[]{:S(2)}, u32[]{:S(2)}) collective-permute-start(bf16[256,256]{0,1:T(8,128)(2,1)S(1)} %get-tuple-element.308), channel_id=1, source_target_pairs={{0,1},{2,3},{4,5},{6,7},{8,9},{10,11},{12,13},{14,15},{16,17},{18,... | collective-permute-start | bytes 393224 | tf_op jit(solution)/shard_map/while/body/eval_jaxpr/ppermute | solution.py:12
  93.4 6.9 %collective-permute-start.2 = (bf16[256,256]{0,1:T(8,128)(2,1)S(1)}, bf16[256,256]{0,1:T(8,128)(2,1)S(1)}, u32[]{:S(2)}, u32[]{:S(2)}) collective-permute-start(bf16[256,256]{0,1:T(8,128)(2,1)S(1)} %get-tuple-element.309), channel_id=1, source_target_pairs={{0,16},{1,17},{2,18},{3,19},{4,20},{5,21},{6,22},{7,23},{8,24},{9,... | collective-permute-start | bytes 393224 | tf_op jit(solution)/shard_map/while/body/eval_jaxpr/ppermute | solution.py:12
  100.3 10.6 %collective-permute-start = (bf16[256,256]{0,1:T(8,128)(2,1)S(1)}, bf16[256,256]{0,1:T(8,128)(2,1)S(1)}, u32[]{:S(2)}, u32[]{:S(2)}) collective-permute-start(bf16[256,256]{0,1:T(8,128)(2,1)S(1)} %get-tuple-element.307), channel_id=1, source_target_pairs={{0,2},{2,4},{4,6},{6,8},{8,10},{10,12},{12,14},{1,3},{3,5},{5,7},{... | collective-permute-start | bytes 393224 | tf_op jit(solution)/shard_map/while/body/eval_jaxpr/ppermute | solution.py:12
  105.2 5.7 %collective-permute-start.1 = (bf16[256,256]{0,1:T(8,128)(2,1)S(1)}, bf16[256,256]{0,1:T(8,128)(2,1)S(1)}, u32[]{:S(2)}, u32[]{:S(2)}) collective-permute-start(bf16[256,256]{0,1:T(8,128)(2,1)S(1)} %get-tuple-element.308), channel_id=1, source_target_pairs={{0,1},{2,3},{4,5},{6,7},{8,9},{10,11},{12,13},{14,15},{16,17},{18,... | collective-permute-start | bytes 393224 | tf_op jit(solution)/shard_map/while/body/eval_jaxpr/ppermute | solution.py:12
  106.6 6.9 %collective-permute-start.2 = (bf16[256,256]{0,1:T(8,128)(2,1)S(1)}, bf16[256,256]{0,1:T(8,128)(2,1)S(1)}, u32[]{:S(2)}, u32[]{:S(2)}) collective-permute-start(bf16[256,256]{0,1:T(8,128)(2,1)S(1)} %get-tuple-element.309), channel_id=1, source_target_pairs={{0,16},{1,17},{2,18},{3,19},{4,20},{5,21},{6,22},{7,23},{8,24},{9,... | collective-permute-start | bytes 393224 | tf_op jit(solution)/shard_map/while/body/eval_jaxpr/ppermute | solution.py:12
  113.5 7.6 %collective-permute-start = (bf16[256,256]{0,1:T(8,128)(2,1)S(1)}, bf16[256,256]{0,1:T(8,128)(2,1)S(1)}, u32[]{:S(2)}, u32[]{:S(2)}) collective-permute-start(bf16[256,256]{0,1:T(8,128)(2,1)S(1)} %get-tuple-element.307), channel_id=1, source_target_pairs={{0,2},{2,4},{4,6},{6,8},{8,10},{10,12},{12,14},{1,3},{3,5},{5,7},{... | collective-permute-start | bytes 393224 | tf_op jit(solution)/shard_map/while/body/eval_jaxpr/ppermute | solution.py:12
  115.4 5.7 %collective-permute-start.1 = (bf16[256,256]{0,1:T(8,128)(2,1)S(1)}, bf16[256,256]{0,1:T(8,128)(2,1)S(1)}, u32[]{:S(2)}, u32[]{:S(2)}) collective-permute-start(bf16[256,256]{0,1:T(8,128)(2,1)S(1)} %get-tuple-element.308), channel_id=1, source_target_pairs={{0,1},{2,3},{4,5},{6,7},{8,9},{10,11},{12,13},{14,15},{16,17},{18,... | collective-permute-start | bytes 393224 | tf_op jit(solution)/shard_map/while/body/eval_jaxpr/ppermute | solution.py:12
  116.7 6.9 %collective-permute-start.2 = (bf16[256,256]{0,1:T(8,128)(2,1)S(1)}, bf16[256,256]{0,1:T(8,128)(2,1)S(1)}, u32[]{:S(2)}, u32[]{:S(2)}) collective-permute-start(bf16[256,256]{0,1:T(8,128)(2,1)S(1)} %get-tuple-element.309), channel_id=1, source_target_pairs={{0,16},{1,17},{2,18},{3,19},{4,20},{5,21},{6,22},{7,23},{8,24},{9,... | collective-permute-start | bytes 393224 | tf_op jit(solution)/shard_map/while/body/eval_jaxpr/ppermute | solution.py:12
  123.7 10.6 %collective-permute-start = (bf16[256,256]{0,1:T(8,128)(2,1)S(1)}, bf16[256,256]{0,1:T(8,128)(2,1)S(1)}, u32[]{:S(2)}, u32[]{:S(2)}) collective-permute-start(bf16[256,256]{0,1:T(8,128)(2,1)S(1)} %get-tuple-element.307), channel_id=1, source_target_pairs={{0,2},{2,4},{4,6},{6,8},{8,10},{10,12},{12,14},{1,3},{3,5},{5,7},{... | collective-permute-start | bytes 393224 | tf_op jit(solution)/shard_map/while/body/eval_jaxpr/ppermute | solution.py:12
  128.6 5.7 %collective-permute-start.1 = (bf16[256,256]{0,1:T(8,128)(2,1)S(1)}, bf16[256,256]{0,1:T(8,128)(2,1)S(1)}, u32[]{:S(2)}, u32[]{:S(2)}) collective-permute-start(bf16[256,256]{0,1:T(8,128)(2,1)S(1)} %get-tuple-element.308), channel_id=1, source_target_pairs={{0,1},{2,3},{4,5},{6,7},{8,9},{10,11},{12,13},{14,15},{16,17},{18,... | collective-permute-start | bytes 393224 | tf_op jit(solution)/shard_map/while/body/eval_jaxpr/ppermute | solution.py:12
  129.9 6.9 %collective-permute-start.2 = (bf16[256,256]{0,1:T(8,128)(2,1)S(1)}, bf16[256,256]{0,1:T(8,128)(2,1)S(1)}, u32[]{:S(2)}, u32[]{:S(2)}) collective-permute-start(bf16[256,256]{0,1:T(8,128)(2,1)S(1)} %get-tuple-element.309), channel_id=1, source_target_pairs={{0,16},{1,17},{2,18},{3,19},{4,20},{5,21},{6,22},{7,23},{8,24},{9,... | collective-permute-start | bytes 393224 | tf_op jit(solution)/shard_map/while/body/eval_jaxpr/ppermute | solution.py:12
  136.9 7.6 %collective-permute-start = (bf16[256,256]{0,1:T(8,128)(2,1)S(1)}, bf16[256,256]{0,1:T(8,128)(2,1)S(1)}, u32[]{:S(2)}, u32[]{:S(2)}) collective-permute-start(bf16[256,256]{0,1:T(8,128)(2,1)S(1)} %get-tuple-element.307), channel_id=1, source_target_pairs={{0,2},{2,4},{4,6},{6,8},{8,10},{10,12},{12,14},{1,3},{3,5},{5,7},{... | collective-permute-start | bytes 393224 | tf_op jit(solution)/shard_map/while/body/eval_jaxpr/ppermute | solution.py:12
  138.8 5.7 %collective-permute-start.1 = (bf16[256,256]{0,1:T(8,128)(2,1)S(1)}, bf16[256,256]{0,1:T(8,128)(2,1)S(1)}, u32[]{:S(2)}, u32[]{:S(2)}) collective-permute-start(bf16[256,256]{0,1:T(8,128)(2,1)S(1)} %get-tuple-element.308), channel_id=1, source_target_pairs={{0,1},{2,3},{4,5},{6,7},{8,9},{10,11},{12,13},{14,15},{16,17},{18,... | collective-permute-start | bytes 393224 | tf_op jit(solution)/shard_map/while/body/eval_jaxpr/ppermute | solution.py:12
  140.1 6.9 %collective-permute-start.2 = (bf16[256,256]{0,1:T(8,128)(2,1)S(1)}, bf16[256,256]{0,1:T(8,128)(2,1)S(1)}, u32[]{:S(2)}, u32[]{:S(2)}) collective-permute-start(bf16[256,256]{0,1:T(8,128)(2,1)S(1)} %get-tuple-element.309), channel_id=1, source_target_pairs={{0,16},{1,17},{2,18},{3,19},{4,20},{5,21},{6,22},{7,23},{8,24},{9,... | collective-permute-start | bytes 393224 | tf_op jit(solution)/shard_map/while/body/eval_jaxpr/ppermute | solution.py:12
  147.1 9.9 %collective-permute-start = (bf16[256,256]{0,1:T(8,128)(2,1)S(1)}, bf16[256,256]{0,1:T(8,128)(2,1)S(1)}, u32[]{:S(2)}, u32[]{:S(2)}) collective-permute-start(bf16[256,256]{0,1:T(8,128)(2,1)S(1)} %get-tuple-element.307), channel_id=1, source_target_pairs={{0,2},{2,4},{4,6},{6,8},{8,10},{10,12},{12,14},{1,3},{3,5},{5,7},{... | collective-permute-start | bytes 393224 | tf_op jit(solution)/shard_map/while/body/eval_jaxpr/ppermute | solution.py:12
  151.2 5.7 %collective-permute-start.1 = (bf16[256,256]{0,1:T(8,128)(2,1)S(1)}, bf16[256,256]{0,1:T(8,128)(2,1)S(1)}, u32[]{:S(2)}, u32[]{:S(2)}) collective-permute-start(bf16[256,256]{0,1:T(8,128)(2,1)S(1)} %get-tuple-element.308), channel_id=1, source_target_pairs={{0,1},{2,3},{4,5},{6,7},{8,9},{10,11},{12,13},{14,15},{16,17},{18,... | collective-permute-start | bytes 393224 | tf_op jit(solution)/shard_map/while/body/eval_jaxpr/ppermute | solution.py:12
  152.6 6.9 %collective-permute-start.2 = (bf16[256,256]{0,1:T(8,128)(2,1)S(1)}, bf16[256,256]{0,1:T(8,128)(2,1)S(1)}, u32[]{:S(2)}, u32[]{:S(2)}) collective-permute-start(bf16[256,256]{0,1:T(8,128)(2,1)S(1)} %get-tuple-element.309), channel_id=1, source_target_pairs={{0,16},{1,17},{2,18},{3,19},{4,20},{5,21},{6,22},{7,23},{8,24},{9,... | collective-permute-start | bytes 393224 | tf_op jit(solution)/shard_map/while/body/eval_jaxpr/ppermute | solution.py:12
  159.5 7.6 %collective-permute-start = (bf16[256,256]{0,1:T(8,128)(2,1)S(1)}, bf16[256,256]{0,1:T(8,128)(2,1)S(1)}, u32[]{:S(2)}, u32[]{:S(2)}) collective-permute-start(bf16[256,256]{0,1:T(8,128)(2,1)S(1)} %get-tuple-element.307), channel_id=1, source_target_pairs={{0,2},{2,4},{4,6},{6,8},{8,10},{10,12},{12,14},{1,3},{3,5},{5,7},{... | collective-permute-start | bytes 393224 | tf_op jit(solution)/shard_map/while/body/eval_jaxpr/ppermute | solution.py:12
  161.4 5.7 %collective-permute-start.1 = (bf16[256,256]{0,1:T(8,128)(2,1)S(1)}, bf16[256,256]{0,1:T(8,128)(2,1)S(1)}, u32[]{:S(2)}, u32[]{:S(2)}) collective-permute-start(bf16[256,256]{0,1:T(8,128)(2,1)S(1)} %get-tuple-element.308), channel_id=1, source_target_pairs={{0,1},{2,3},{4,5},{6,7},{8,9},{10,11},{12,13},{14,15},{16,17},{18,... | collective-permute-start | bytes 393224 | tf_op jit(solution)/shard_map/while/body/eval_jaxpr/ppermute | solution.py:12
  162.7 6.9 %collective-permute-start.2 = (bf16[256,256]{0,1:T(8,128)(2,1)S(1)}, bf16[256,256]{0,1:T(8,128)(2,1)S(1)}, u32[]{:S(2)}, u32[]{:S(2)}) collective-permute-start(bf16[256,256]{0,1:T(8,128)(2,1)S(1)} %get-tuple-element.309), channel_id=1, source_target_pairs={{0,16},{1,17},{2,18},{3,19},{4,20},{5,21},{6,22},{7,23},{8,24},{9,... | collective-permute-start | bytes 393224 | tf_op jit(solution)/shard_map/while/body/eval_jaxpr/ppermute | solution.py:12
where the time goes:
time: 174 us; the launch traced here: 172 us
  starting transfers between devices  112 us (64%)
  waiting for transfers between devices  32.2 us (19%)
  local copies, waits for them, and re-layouts  16.3 us (9%)
  matrix products  10.6 us (6%)
    ppermute x39, starting transfers between devices, shifted(): return lax.ppermute(block, axis, route)  112 us
    ppermute x39, waiting for transfers between devices, shifted(): return lax.ppermute(block, axis, route)  32.2 us
    dot_general x4, matrix products, source_part(): return jnp.dot(op_source, block, preferred_element_type=jnp.float32)  7.35 us
    slice x1, local copies, waits for them, and re-layouts, shards(): op_source = local_op[:, 3 * trace:]  4.09 us
  transfers between devices with their start and end apart: 39, of which 13 were waited for; matrix products, arithmetic and copies ran while one was open for 0% of the time, Pallas kernels for 0%

commit v1 on v0

v1 whole, which is shorter than its diff:
```python
import functools
import jax
import jax.numpy as jnp
from jax import lax
from jax.experimental import pallas as pl
from jax.experimental.pallas import tpu as pltpu
from jax.sharding import PartitionSpec as P

STREAMS = 4
REPEAT = 4
VMEM = pl.BlockSpec(memory_space=pltpu.VMEM)
SMEM = pl.BlockSpec(memory_space=pltpu.SMEM)
HBM = pl.BlockSpec(memory_space=pltpu.HBM)
AXES = ("depth", "gx", "gy")
f32 = jnp.float32
bf16 = jnp.bfloat16


def dot(a, b):
    return jnp.dot(a, b, preferred_element_type=f32)


def shaped(shape, dtype=bf16):
    return jax.ShapeDtypeStruct(shape, dtype)


def call(kernel, ins, outs, out_specs, mib, flops, nbytes, scratch=(), aliases=None):
    return pl.pallas_call(
        kernel,
        out_shape=outs,
        in_specs=ins,
        out_specs=out_specs,
        scratch_shapes=list(scratch),
        input_output_aliases=aliases or {},
        compiler_params=pltpu.CompilerParams(vmem_limit_bytes=mib << 20),
        cost_estimate=pl.CostEstimate(flops=flops, bytes_accessed=nbytes, transcendentals=0),
    )


def route(sizes, axis, tick):
    nd, nx, ny = sizes
    pairs = []
    for d in range(nd):
        for i in range(nx):
            for j in range(ny):
                group = j // 2
                at, to = [d, i, group], [d, i, group]
                to[axis] += 1
                if to[axis] < (nd, nx, ny // 2)[axis] and (sum(at) - tick) % (REPEAT if axis == 1 else 8) == 0:
                    end = (to[0] * nx + to[1]) * ny + 2 * to[2] + j % 2
                    pairs.append(((d * nx + i) * ny + j, end))
    return pairs


def fetch_kernel(rows, op_ref, t_ref):
    t_ref[...] = op_ref[:rows, :rows]


def give_kernel(rows, half, parity_ref, op_ref, src_ref, give_ref):
    other = pl.ds(pl.multiple_of((1 - parity_ref[0]) * half, 128), half)
    step = rows // 3

    def body(n, _):
        part = pl.ds(pl.multiple_of(n * step, step), step)
        give_ref[part, :] = dot(op_ref[part, rows:], src_ref[:, other]).astype(bf16)
        return 0

    lax.fori_loop(0, 3, body, 0)


def own_kernel(half, parity_ref, op_ref, src_ref, t_ref, got_ref, both_ref, s_ref):
    trows = t_ref.shape[0]
    step = trows // 3
    mine = pl.ds(pl.multiple_of(parity_ref[0] * half, 128), half)

    def body(n, _):
        rows = pl.ds(pl.multiple_of(n * step, step), step)
        s_ref[rows, :] = dot(op_ref[rows, trows:], src_ref[:, mine])
        both_ref[parity_ref[0], rows, :] = t_ref[rows, :]
        both_ref[1 - parity_ref[0], rows, :] = got_ref[rows, :]
        return 0

    lax.fori_loop(0, 3, body, 0)


def pair_sources(parity_ref, s_ref, given_ref, rows, columns):
    own, given = s_ref[rows, columns], given_ref[rows, columns].astype(f32)
    even = parity_ref[0] == 0
    return jnp.where(even, own, given), jnp.where(even, given, own)


def lower_side(op, rows, trace, total, parts):
    for n, part in enumerate(parts):
        if part is not None:
            total += dot(op[rows, n * trace : (n + 1) * trace], part)
    return total


def halves(ref, trace):
    return (None, None) if ref is None else (ref[:trace, :], ref[trace:, :])


def paired(ref, trace, slot):
    if ref is None:
        return None, None
    at = 2 * slot * trace
    return ref[at : at + trace, :], ref[at + trace : at + 2 * trace, :]


def tick_kernel(tick, trace, columns, slot, moving, has_row, level_ref, parity_ref, both_ref, s_ref, given_ref, turn_ref, *refs):
    del turn_ref
    refs = list(refs)
    x_in = refs.pop(0) if moving else None
    z_in = refs.pop(0) if moving else None
    y_in = refs.pop(0) if moving and has_row else None
    first = refs.pop(0) if slot else None
    x_out, z_out, mid_out = refs[:3]

    @pl.when(level_ref[0] == tick)
    def _():
        xa, xb = halves(x_in, trace)
        za, zb = paired(z_in, trace, slot)
        ya = None if y_in is None else y_in[...]
        sa, sb = pair_sources(parity_ref, s_ref, given_ref, slice(0, 3 * trace), columns)
        every = slice(0, 3 * trace)
        a = lower_side(both_ref.at[0], every, trace, sa, (xa, ya, za)).astype(bf16)
        mid = a[trace : 2 * trace]
        b = lower_side(both_ref.at[1], every, trace, sb, (xb, None, zb))
        b = lower_side(both_ref.at[1], every, trace, b, (None, mid, None)).astype(bf16)
        x_out[:trace, :] = a[:trace]
        x_out[trace:, :] = b[:trace]
        if slot:
            z_out[: 2 * trace, :] = first[...]
        z_out[2 * slot * trace : (2 * slot + 1) * trace, :] = a[2 * trace :]
        z_out[(2 * slot + 1) * trace : (2 * slot + 2) * trace, :] = b[2 * trace :]
        mid_out[...] = mid
        if has_row:
            refs[3][...] = b[trace : 2 * trace]


def last_kernel(top, trace, width, base, has_row, level_ref, parity_ref, both_ref, s_ref, given_ref, turn_ref, *refs):
    del turn_ref
    refs = list(refs)
    own_ref, give_ref = refs[-2:]
    even = parity_ref[0] == 0
    zero = jnp.zeros((trace, width), bf16)

    def put(n, slot, a, b):
        rows = slice(n * trace, (n + 1) * trace)
        cols = slice(slot * width, (slot + 1) * width)
        own_ref[rows, cols] = jnp.where(even, a, b)
        give_ref[rows, cols] = jnp.where(even, b, a)

    for tick in range(top + 1):
        z_in = refs.pop(0) if tick else None
        xs = [refs.pop(0) for _ in range(2)] if tick else [None] * 2
        ys = [refs.pop(0) for _ in range(2)] if tick and has_row else [None] * 2
        mids = [refs.pop(0) for _ in range(2)] if tick < top else [None] * 2

        @pl.when(level_ref[0] == tick)
        def _():
            for slot in range(2):
                xa, xb = halves(xs[slot], trace)
                za, zb = paired(z_in, trace, slot)
                ya = None if ys[slot] is None else ys[slot][...]
                if mids[slot] is None:
                    rows = slice(trace, 2 * trace)
                    start = base + slot * width
                    sa, _ = pair_sources(parity_ref, s_ref, given_ref, rows, slice(start, start + width))
                    yb = lower_side(both_ref.at[0], rows, trace, sa, (xa, ya, za)).astype(bf16)
                else:
                    yb = mids[slot][...]
                put(0, slot, zero if xa is None else xa, zero if xb is None else xb)
                put(1, slot, zero if ya is None else ya, yb)
                put(2, slot, zero if za is None else za, zero if zb is None else zb)


def solve_kernel(rows, half, base, side, parity_ref, op_ref, src_ref, in_ref, out_in, out_ref, token_ref, buf, sem):
    del out_in
    width = buf.shape[1]
    at = parity_ref[0] if side == 0 else 1 - parity_ref[0]
    columns = pl.ds(pl.multiple_of(at * half + base, 128), width)
    step = buf.shape[0] // 3

    def body(n, _):
        local = pl.ds(pl.multiple_of(n * step, step), step)
        below = pl.ds(pl.multiple_of(rows + n * step, step), step)
        total = dot(op_ref[below, rows:], src_ref[:, columns])
        total += dot(op_ref[below, :rows], in_ref[...])
        buf[local, :] = total.astype(bf16)
        return 0

    lax.fori_loop(0, 3, body, 0)
    copy = pltpu.make_async_copy(buf, out_ref.at[:, columns], sem)
    copy.start()
    token_ref[...] = jnp.zeros(token_ref.shape, token_ref.dtype)
    copy.wait()


def room_kernel(out_ref):
    del out_ref


def shards(sizes, operator, sources):
    op = operator[0, 0, 0]
    src = sources[0, 0, 0]
    inner, columns = src.shape
    trace = (op.shape[0] - inner) // 3
    rows = 3 * trace
    half = columns // 2
    width = half // STREAMS
    nd, nx, ny = sizes
    top = nd + nx + ny // 2 - 3
    has_row = ny > 2
    row = lax.axis_index("gy")
    level = lax.axis_index("depth") + lax.axis_index("gx") + (row >> 1)
    level = level.astype(jnp.int32).reshape(1)
    parity = (row & 1).astype(jnp.int32).reshape(1)
    op, src, level, parity = lax.optimization_barrier((op, src, level, parity))
    swap = [(j, j ^ 1) for j in range(ny)]

    t = call(functools.partial(fetch_kernel, rows), [VMEM], shaped((rows, rows)), VMEM, 1, 0, 0)(op)
    got = lax.ppermute(t, "gy", swap)
    give = call(
        functools.partial(give_kernel, rows, half), [SMEM, VMEM, VMEM], shaped((rows, half)), VMEM, 4, 0, 0
    )(parity, op, src)
    given = lax.ppermute(give, "gy", swap)
    both, s = call(
        functools.partial(own_kernel, half), [SMEM] + [VMEM] * 4,
        [shaped((2, rows, rows)), shaped((rows, half), f32)], [VMEM] * 2, 4, 0, 0,
    )(parity, op, src, t, got)
    out = call(room_kernel, [], shaped((inner, columns)), HBM, 1, 0, 0)()

    turn = given
    xs = [[] for _ in range(STREAMS)]
    ys = [[] for _ in range(STREAMS)]
    zs = [[] for _ in range(STREAMS // 2)]
    mids = [[] for _ in range(STREAMS)]
    for tick in range(top):
        for n in range(STREAMS):
            slot = n % 2
            cols = slice(n * width, (n + 1) * width)
            outs = [shaped((2 * trace, width)), shaped((2 * (slot + 1) * trace, width)), shaped((trace, width))]
            outs += [shaped((trace, width))] * has_row
            ins = [turn]
            if tick:
                ins += [xs[n][-1], zs[n // 2][tick - 1]]
                ins += [ys[n][-1]] if has_row else []
            if slot:
                ins.append(pair)
            sent = call(
                functools.partial(tick_kernel, tick, trace, cols, slot, tick > 0, has_row),
                [SMEM] * 2 + [VMEM] * (3 + len(ins)), outs, [VMEM] * len(outs), 4, 0, 0,
            )(level, parity, both, s, given, *ins)
            pair, turn = sent[1:3]
            mids[n].append(turn)
            xs[n].append(lax.ppermute(sent[0], AXES, route(sizes, 1, tick)))
            if has_row:
                ys[n].append(lax.ppermute(sent[3], AXES, route(sizes, 2, tick)))
            if slot:
                zs[n // 2].append(lax.ppermute(pair, AXES, route(sizes, 0, tick)))
    for p in range(STREAMS // 2):
        ins = []
        for tick in range(top + 1):
            ins += [zs[p][tick - 1]] if tick else []
            for part in (xs, ys) if has_row else (xs,):
                ins += [part[2 * p + slot][tick - 1] for slot in range(2)] if tick else []
            ins += [mids[2 * p + slot][tick] for slot in range(2)] if tick < top else []
        base = 2 * p * width
        mine, other = call(
            functools.partial(last_kernel, top, trace, width, base, has_row),
            [SMEM] * 2 + [VMEM] * (4 + len(ins)), [shaped((rows, 2 * width))] * 2, [VMEM] * 2, 4, 0, 0,
        )(level, parity, both, s, given, turn, *ins)
        back = lax.ppermute(other, "gy", swap)
        for side, part in enumerate((mine, back)):
            out, turn = call(
                functools.partial(solve_kernel, rows, half, base, side), [SMEM] + [VMEM] * 3 + [HBM],
                [shaped((inner, columns)), shaped((8, 128), f32)], [HBM, VMEM], 4, 0, 0,
                scratch=[pltpu.VMEM((inner, 2 * width), bf16), pltpu.SemaphoreType.DMA], aliases={4: 0},
            )(parity, op, src, part, out)
    return out[None, None, None]


def solution(mesh):
    spec = P("depth", "gx", "gy", None, None)
    sizes = tuple(mesh.shape[a] for a in AXES)
    return jax.shard_map(
        functools.partial(shards, sizes), mesh=mesh, in_specs=(spec, spec), out_specs=spec, check_vma=False
    )
```

time: 174 us -> 138 us (0.79)
  the two profiles are of different devices: /device:TPU:0 before, /device:TPU:31 now
where the time goes in v1:
time: 138 us; the launch traced here: 137 us
  waiting for transfers between devices  62.4 us (45%)
  starting transfers between devices  55.9 us (41%)
  Pallas kernels  12.8 us (9%)
  local copies, waits for them, and re-layouts  5.26 us (4%)
    ppermute x32, waiting for transfers between devices, shards(): xs[n].append(lax.ppermute(sent[0], AXES, route(sizes, 1, tick)))  60.1 us
    ppermute x32, starting transfers between devices, shards(): xs[n].append(lax.ppermute(sent[0], AXES, route(sizes, 1, tick)))  26.4 us
    ppermute x2, starting transfers between devices, shards(): back = lax.ppermute(other, 'gy', swap)  16 us
    ppermute x16, starting transfers between devices, shards(): zs[n // 2].append(lax.ppermute(pair, AXES, route(sizes, 0, tick)))  12 us
    pallas_call x4, Pallas kernels, shards(): call(functools.partial(solve_kernel, rows, half, base, side), [SMEM] + [V...  9.42 us
    unnamed x8, local copies, waits for them, and re-layouts  5.26 us
  transfers between devices with their start and end apart: 52, of which 10 were waited for; matrix products, arithmetic and copies ran while one was open for 0% of the time, Pallas kernels for 7%

profile of v1, /device:TPU:31, one launch (start us, length us, event | category | flops | bytes accessed | tf_op | source)
XLA Modules:
  0.0 137.4 jit_solution(10384856492112933553)
XLA Ops:
  0.0 2.3 %copy-done = bf16[1,1,1,1536,1536]{4,3,2,1,0:T(8,128)(2,1)S(1)} copy-done((bf16[1,1,1,1536,1536]{4,3,2,1,0:T(8,128)(2,1)S(1)}, bf16[1,1,1,1536,1536]{4,3,2,1,0:T(8,128)(2,1)}, u32[]{:S(2)}) %copy-start) | copy-done | bytes 4718616
  2.4 0.7 collective-permute-start
  3.2 1.5 %copy-done.1 = bf16[1,1,1,1536,1536]{4,3,2,1,0:T(8,128)(2,1)S(1)} copy-done((bf16[1,1,1,1536,1536]{4,3,2,1,0:T(8,128)(2,1)S(1)}, bf16[1,1,1,1536,1536]{4,3,2,1,0:T(8,128)(2,1)}, u32[]{:S(2)}) %copy-start.1) | copy-done | bytes 4718616
  4.7 1.4 %copy-done.2 = bf16[1,1,1,768,1024]{4,3,2,1,0:T(8,128)(2,1)S(1)} copy-done((bf16[1,1,1,768,1024]{4,3,2,1,0:T(8,128)(2,1)S(1)}, bf16[1,1,1,768,1024]{4,3,2,1,0:T(8,128)(2,1)}, u32[]{:S(2)}) %copy-start.2) | copy-done | bytes 1572888
  6.1 1.1 shard_map.30
  7.2 0.7 collective-permute-start.1
  8.0 1.2 shard_map.29
  9.2 0.7 collective-permute-done.1.given_ref.turn_ref
  10.5 0.7 collective-permute-start.2
  11.2 0.7 collective-permute-start.4
  11.9 0.7 collective-permute-start.6
  12.7 0.7 collective-permute-start.9
  13.4 0.7 collective-permute-start.5
  14.0 0.7 collective-permute-start.7
  14.7 0.7 collective-permute-start.8
  15.4 0.7 collective-permute-start.10
  16.1 0.7 collective-permute-start.12
  16.9 0.7 collective-permute-start.15
  17.6 0.7 collective-permute-start.11
  18.3 0.7 collective-permute-start.13
  18.9 0.7 collective-permute-start.14
  19.6 0.7 collective-permute-start.16
  20.4 0.7 collective-permute-start.18
  21.1 0.7 collective-permute-start.21
  21.8 0.7 collective-permute-start.17
  22.5 0.7 collective-permute-start.19
  23.2 1.3 collective-permute-start.20
  24.5 1.3 collective-permute-start.22
  25.8 0.7 collective-permute-start.24
  26.5 23.7 %collective-permute-done.20.refs_0_.refs_18_ = bf16[512,128]{1,0:T(8,128)(2,1)S(1)} collective-permute-done((bf16[512,128]{1,0:T(8,128)(2,1)S(1)}, bf16[512,128]{1,0:T(8,128)(2,1)S(1)}, u32[]{:S(2)}, u32[]{:S(2)}) %collective-permute-start.20) | collective-permute-done | bytes 131104 | tf_op jit(solution)/shard_map/ppermute | solution.py:257
  50.2 4.0 %collective-permute-done.22.refs_0_.refs_19_ = bf16[512,128]{1,0:T(8,128)(2,1)S(1)} collective-permute-done((bf16[512,128]{1,0:T(8,128)(2,1)S(1)}, bf16[512,128]{1,0:T(8,128)(2,1)S(1)}, u32[]{:S(2)}, u32[]{:S(2)}) %collective-permute-start.22) | collective-permute-done | bytes 131104 | tf_op jit(solution)/shard_map/ppermute | solution.py:257
  54.9 1.3 collective-permute-start.23
  56.2 1.3 collective-permute-start.25
  57.5 0.7 collective-permute-start.26
  58.2 2.8 %collective-permute-done.23.refs_0_.refs_18_ = bf16[512,128]{1,0:T(8,128)(2,1)S(1)} collective-permute-done((bf16[512,128]{1,0:T(8,128)(2,1)S(1)}, bf16[512,128]{1,0:T(8,128)(2,1)S(1)}, u32[]{:S(2)}, u32[]{:S(2)}) %collective-permute-start.23) | collective-permute-done | bytes 131104 | tf_op jit(solution)/shard_map/ppermute | solution.py:257
  61.7 2.0 %collective-permute-done.25.refs_0_.refs_19_ = bf16[512,128]{1,0:T(8,128)(2,1)S(1)} collective-permute-done((bf16[512,128]{1,0:T(8,128)(2,1)S(1)}, bf16[512,128]{1,0:T(8,128)(2,1)S(1)}, u32[]{:S(2)}, u32[]{:S(2)}) %collective-permute-start.25) | collective-permute-done | bytes 131104 | tf_op jit(solution)/shard_map/ppermute | solution.py:257
  64.4 0.7 collective-permute-start.33
  65.1 0.7 collective-permute-start.29
  65.7 0.7 collective-permute-start.31
  66.4 0.7 collective-permute-start.32
  67.1 0.7 collective-permute-start.34
  67.8 0.7 collective-permute-start.36
  68.6 0.7 collective-permute-start.39
  69.3 0.7 collective-permute-start.35
  70.0 0.7 collective-permute-start.37
  70.6 0.7 collective-permute-start.38
  72.1 0.7 collective-permute-start.42
  73.5 1.3 collective-permute-start.44
  74.8 0.7 collective-permute-start.43
  75.5 1.3 collective-permute-start.46
  76.8 1.3 collective-permute-start.45
  78.1 21.1 %collective-permute-done.46.refs_39_ = bf16[512,128]{1,0:T(8,128)(2,1)S(1)} collective-permute-done((bf16[512,128]{1,0:T(8,128)(2,1)S(1)}, bf16[512,128]{1,0:T(8,128)(2,1)S(1)}, u32[]{:S(2)}, u32[]{:S(2)}) %collective-permute-start.46) | collective-permute-done | bytes 131104 | tf_op jit(solution)/shard_map/ppermute | solution.py:257
  99.3 3.7 %collective-permute-done.45.refs_38_ = bf16[512,128]{1,0:T(8,128)(2,1)S(1)} collective-permute-done((bf16[512,128]{1,0:T(8,128)(2,1)S(1)}, bf16[512,128]{1,0:T(8,128)(2,1)S(1)}, u32[]{:S(2)}, u32[]{:S(2)}) %collective-permute-start.45) | collective-permute-done | bytes 131104 | tf_op jit(solution)/shard_map/ppermute | solution.py:257
  103.0 1.4 %collective-permute-done.44.refs_37_ = bf16[1024,128]{1,0:T(8,128)(2,1)S(1)} collective-permute-done((bf16[1024,128]{1,0:T(8,128)(2,1)S(1)}, bf16[1024,128]{1,0:T(8,128)(2,1)S(1)}, u32[]{:S(2)}, u32[]{:S(2)}) %collective-permute-start.44) | collective-permute-done | bytes 262176 | tf_op jit(solution)/shard_map/ppermute | solution.py:261
  104.7 15.2 %collective-permute-start.47 = (bf16[768,256]{1,0:T(8,128)(2,1)S(1)}, bf16[768,256]{1,0:T(8,128)(2,1)S(1)}, u32[]{:S(2)}, u32[]{:S(2)}) collective-permute-start(bf16[768,256]{1,0:T(8,128)(2,1)S(1)} %get-tuple-element.215), channel_id=1, source_target_pairs={{0,1},{1,0},{2,3},{3,2},{4,5},{5,4},{6,7},{7,6},{8,9},{9,8},{10,11... | collective-permute-start | bytes 1179656 | tf_op jit(solution)/shard_map/ppermute | solution.py:274
  119.9 1.3 collective-permute-start.48
  121.2 1.3 collective-permute-start.50
  122.5 1.3 collective-permute-start.49
  123.8 2.5 %shard_map.65 = (bf16[768,1024]{1,0:T(8,128)(2,1)}, f32[8,128]{1,0:T(8,128)}) custom-call(s32[1]{0:T(128)} %bitcast.3.parity_ref, bf16[1536,1536]{1,0:T(8,128)(2,1)S(1)} %bitcast.8, bf16[768,1024]{1,0:T(8,128)(2,1)S(1)} %bitcast.14, bf16[768,256]{1,0:T(8,128)(2,1)S(1)} %get-tuple-element.216.in_ref, ...), custom_call_target="tpu_custom_call", output_to_operand_aliasing={{0}: (4, {})} | custom-call | tf_op jit(solution)/shard_map/pallas_call | solution.py:276
  126.3 1.9 %shard_map.66 = (bf16[768,1024]{1,0:T(8,128)(2,1)}, f32[8,128]{1,0:T(8,128)S(1)}) custom-call(s32[1]{0:T(128)} %bitcast.3.parity_ref, bf16[1536,1536]{1,0:T(8,128)(2,1)S(1)} %bitcast.9, bf16[768,1024]{1,0:T(8,128)(2,1)S(1)} %bitcast.15, bf16[768,256]{1,0:T(8,128)(2,1)S(1)} %collective-permute-done.47.in_ref, ...), custom_call_target="tpu_custom_call", output_to_operand_aliasing={{0}: (4, {})} | custom-call | tf_op jit(solution)/shard_map/pallas_call | solution.py:276
  128.2 2.7 %collective-permute-done.49.refs_38_ = bf16[512,128]{1,0:T(8,128)(2,1)S(1)} collective-permute-done((bf16[512,128]{1,0:T(8,128)(2,1)S(1)}, bf16[512,128]{1,0:T(8,128)(2,1)S(1)}, u32[]{:S(2)}, u32[]{:S(2)}) %collective-permute-start.49) | collective-permute-done | bytes 131104 | tf_op jit(solution)/shard_map/ppermute | solution.py:257
  131.4 0.8 collective-permute-start.51
  132.2 2.5 %shard_map.68 = (bf16[768,1024]{1,0:T(8,128)(2,1)}, f32[8,128]{1,0:T(8,128)}) custom-call(s32[1]{0:T(128)} %bitcast.3.parity_ref, bf16[1536,1536]{1,0:T(8,128)(2,1)S(1)} %bitcast.10, bf16[768,1024]{1,0:T(8,128)(2,1)S(1)} %bitcast.16, bf16[768,256]{1,0:T(8,128)(2,1)S(1)} %get-tuple-element.223.in_ref, ...), custom_call_target="tpu_custom_call", output_to_operand_aliasing={{0}: (4, {})} | custom-call | tf_op jit(solution)/shard_map/pallas_call | solution.py:276
  134.7 2.5 %shard_map.69 = (bf16[768,1024]{1,0:T(8,128)(2,1)}, f32[8,128]{1,0:T(8,128)}) custom-call(s32[1]{0:T(128)} %bitcast.3.parity_ref, bf16[1536,1536]{1,0:T(8,128)(2,1)S(1)} %bitcast.11, bf16[768,1024]{1,0:T(8,128)(2,1)S(1)} %bitcast.17, bf16[768,256]{1,0:T(8,128)(2,1)S(1)} %collective-permute-done.51.in_ref, ...), custom_call_target="tpu_custom_call", output_to_operand_aliasing={{0}: (4, {})} | custom-call | tf_op jit(solution)/shard_map/pallas_call | solution.py:276
  (90 shorter events, 5.3 us)
Async XLA Ops:
  0.0 2.3 %copy-start = (bf16[1,1,1,1536,1536]{4,3,2,1,0:T(8,128)(2,1)S(1)}, bf16[1,1,1,1536,1536]{4,3,2,1,0:T(8,128)(2,1)}, u32[]{:S(2)}) copy-start(bf16[1,1,1,1536,1536]{4,3,2,1,0:T(8,128)(2,1)} %param.2) | copy-start | bytes 14155780
  2.3 2.3 %copy-start.1 = (bf16[1,1,1,1536,1536]{4,3,2,1,0:T(8,128)(2,1)S(1)}, bf16[1,1,1,1536,1536]{4,3,2,1,0:T(8,128)(2,1)}, u32[]{:S(2)}) copy-start(bf16[1,1,1,1536,1536]{4,3,2,1,0:T(8,128)(2,1)} %param.2) | copy-start | bytes 14155780
  2.4 5.5 %collective-permute-start = (bf16[768,768]{1,0:T(8,128)(2,1)S(1)}, bf16[768,768]{1,0:T(8,128)(2,1)S(1)}, u32[]{:S(2)}, u32[]{:S(2)}) collective-permute-start(bf16[768,768]{1,0:T(8,128)(2,1)S(1)} %shard_map.28.t_ref), channel_id=1, source_target_pairs={{0,1},{1,0},{2,3},{3,2},{4,5},{5,4},{6,7},{7,6},{8,9},{9,8},{10,11... | collective-permute-start | bytes 3538952 | tf_op jit(solution)/shard_map/ppermute | solution.py:223
  4.7 1.4 %copy-start.2 = (bf16[1,1,1,768,1024]{4,3,2,1,0:T(8,128)(2,1)S(1)}, bf16[1,1,1,768,1024]{4,3,2,1,0:T(8,128)(2,1)}, u32[]{:S(2)}) copy-start(bf16[1,1,1,768,1024]{4,3,2,1,0:T(8,128)(2,1)} %param.3) | copy-start | bytes 4718596
  6.1 1.9 %copy-start.3 = (bf16[1,1,1,768,1024]{4,3,2,1,0:T(8,128)(2,1)S(1)}, bf16[1,1,1,768,1024]{4,3,2,1,0:T(8,128)(2,1)}, u32[]{:S(2)}) copy-start(bf16[1,1,1,768,1024]{4,3,2,1,0:T(8,128)(2,1)} %param.3) | copy-start | bytes 4718596
  7.2 2.7 %collective-permute-start.1 = (bf16[768,512]{1,0:T(8,128)(2,1)S(1)}, bf16[768,512]{1,0:T(8,128)(2,1)S(1)}, u32[]{:S(2)}, u32[]{:S(2)}) collective-permute-start(bf16[768,512]{1,0:T(8,128)(2,1)S(1)} %shard_map.30), channel_id=1, source_target_pairs={{0,1},{1,0},{2,3},{3,2},{4,5},{5,4},{6,7},{7,6},{8,9},{9,8},{10,11... | collective-permute-start | bytes 2359304 | tf_op jit(solution)/shard_map/ppermute | solution.py:227
  9.9 2.8 %collective-permute-start.3 = (bf16[1024,128]{1,0:T(8,128)(2,1)S(1)}, bf16[1024,128]{1,0:T(8,128)(2,1)S(1)}, u32[]{:S(2)}, u32[]{:S(2)}) collective-permute-start(bf16[1024,128]{1,0:T(8,128)(2,1)S(1)} %get-tuple-element.129), channel_id=1, source_target_pairs={{0,16},{1,17}} | collective-permute-start | bytes 786440 | tf_op jit(solution)/shard_map/ppermute | solution.py:261
  10.5 2.1 %collective-permute-start.2 = (bf16[512,128]{1,0:T(8,128)(2,1)S(1)}, bf16[512,128]{1,0:T(8,128)(2,1)S(1)}, u32[]{:S(2)}, u32[]{:S(2)}) collective-permute-start(bf16[512,128]{1,0:T(8,128)(2,1)S(1)} %get-tuple-element.128), channel_id=1, source_target_pairs={{0,2},{1,3},{8,10},{9,11},{22,24},{23,25}} | collective-permute-start | bytes 393224 | tf_op jit(solution)/shard_map/ppermute | solution.py:257
  11.2 1.4 %collective-permute-start.4 = (bf16[512,128]{1,0:T(8,128)(2,1)S(1)}, bf16[512,128]{1,0:T(8,128)(2,1)S(1)}, u32[]{:S(2)}, u32[]{:S(2)}) collective-permute-start(bf16[512,128]{1,0:T(8,128)(2,1)S(1)} %get-tuple-element.131), channel_id=1, source_target_pairs={{0,2},{1,3},{8,10},{9,11},{22,24},{23,25}} | collective-permute-start | bytes 393224 | tf_op jit(solution)/shard_map/ppermute | solution.py:257
  11.9 4.2 %collective-permute-start.6 = (bf16[1024,128]{1,0:T(8,128)(2,1)S(1)}, bf16[1024,128]{1,0:T(8,128)(2,1)S(1)}, u32[]{:S(2)}, u32[]{:S(2)}) collective-permute-start(bf16[1024,128]{1,0:T(8,128)(2,1)S(1)} %get-tuple-element.135), channel_id=1, source_target_pairs={{0,16},{1,17}} | collective-permute-start | bytes 786440 | tf_op jit(solution)/shard_map/ppermute | solution.py:261
  12.7 4.2 %collective-permute-start.9 = (bf16[1024,128]{1,0:T(8,128)(2,1)S(1)}, bf16[1024,128]{1,0:T(8,128)(2,1)S(1)}, u32[]{:S(2)}, u32[]{:S(2)}) collective-permute-start(bf16[1024,128]{1,0:T(8,128)(2,1)S(1)} %get-tuple-element.141), channel_id=1, source_target_pairs={{2,18},{3,19}} | collective-permute-start | bytes 786440 | tf_op jit(solution)/shard_map/ppermute | solution.py:261
  13.4 2.0 %collective-permute-start.5 = (bf16[512,128]{1,0:T(8,128)(2,1)S(1)}, bf16[512,128]{1,0:T(8,128)(2,1)S(1)}, u32[]{:S(2)}, u32[]{:S(2)}) collective-permute-start(bf16[512,128]{1,0:T(8,128)(2,1)S(1)} %get-tuple-element.134), channel_id=1, source_target_pairs={{0,2},{1,3},{8,10},{9,11},{22,24},{23,25}} | collective-permute-start | bytes 393224 | tf_op jit(solution)/shard_map/ppermute | solution.py:257
  14.0 2.1 %collective-permute-start.7 = (bf16[512,128]{1,0:T(8,128)(2,1)S(1)}, bf16[512,128]{1,0:T(8,128)(2,1)S(1)}, u32[]{:S(2)}, u32[]{:S(2)}) collective-permute-start(bf16[512,128]{1,0:T(8,128)(2,1)S(1)} %get-tuple-element.137), channel_id=1, source_target_pairs={{0,2},{1,3},{8,10},{9,11},{22,24},{23,25}} | collective-permute-start | bytes 393224 | tf_op jit(solution)/shard_map/ppermute | solution.py:257
  14.7 2.1 %collective-permute-start.8 = (bf16[512,128]{1,0:T(8,128)(2,1)S(1)}, bf16[512,128]{1,0:T(8,128)(2,1)S(1)}, u32[]{:S(2)}, u32[]{:S(2)}) collective-permute-start(bf16[512,128]{1,0:T(8,128)(2,1)S(1)} %get-tuple-element.140), channel_id=1, source_target_pairs={{2,4},{3,5},{10,12},{11,13},{16,18},{17,19},{24,26},{25,27}} | collective-permute-start | bytes 393224 | tf_op jit(solution)/shard_map/ppermute | solution.py:257
  15.4 1.5 %collective-permute-start.10 = (bf16[512,128]{1,0:T(8,128)(2,1)S(1)}, bf16[512,128]{1,0:T(8,128)(2,1)S(1)}, u32[]{:S(2)}, u32[]{:S(2)}) collective-permute-start(bf16[512,128]{1,0:T(8,128)(2,1)S(1)} %get-tuple-element.143), channel_id=1, source_target_pairs={{2,4},{3,5},{10,12},{11,13},{16,18},{17,19},{24,26},{25,27}} | collective-permute-start | bytes 393224 | tf_op jit(solution)/shard_map/ppermute | solution.py:257
  16.1 4.2 %collective-permute-start.12 = (bf16[1024,128]{1,0:T(8,128)(2,1)S(1)}, bf16[1024,128]{1,0:T(8,128)(2,1)S(1)}, u32[]{:S(2)}, u32[]{:S(2)}) collective-permute-start(bf16[1024,128]{1,0:T(8,128)(2,1)S(1)} %get-tuple-element.147), channel_id=1, source_target_pairs={{2,18},{3,19}} | collective-permute-start | bytes 786440 | tf_op jit(solution)/shard_map/ppermute | solution.py:261
  16.9 4.2 %collective-permute-start.15 = (bf16[1024,128]{1,0:T(8,128)(2,1)S(1)}, bf16[1024,128]{1,0:T(8,128)(2,1)S(1)}, u32[]{:S(2)}, u32[]{:S(2)}) collective-permute-start(bf16[1024,128]{1,0:T(8,128)(2,1)S(1)} %get-tuple-element.153), channel_id=1, source_target_pairs={{4,20},{5,21}} | collective-permute-start | bytes 786440 | tf_op jit(solution)/shard_map/ppermute | solution.py:261
  17.6 2.0 %collective-permute-start.11 = (bf16[512,128]{1,0:T(8,128)(2,1)S(1)}, bf16[512,128]{1,0:T(8,128)(2,1)S(1)}, u32[]{:S(2)}, u32[]{:S(2)}) collective-permute-start(bf16[512,128]{1,0:T(8,128)(2,1)S(1)} %get-tuple-element.146), channel_id=1, source_target_pairs={{2,4},{3,5},{10,12},{11,13},{16,18},{17,19},{24,26},{25,27}} | collective-permute-start | bytes 393224 | tf_op jit(solution)/shard_map/ppermute | solution.py:257
  18.3 2.1 %collective-permute-start.13 = (bf16[512,128]{1,0:T(8,128)(2,1)S(1)}, bf16[512,128]{1,0:T(8,128)(2,1)S(1)}, u32[]{:S(2)}, u32[]{:S(2)}) collective-permute-start(bf16[512,128]{1,0:T(8,128)(2,1)S(1)} %get-tuple-element.149), channel_id=1, source_target_pairs={{2,4},{3,5},{10,12},{11,13},{16,18},{17,19},{24,26},{25,27}} | collective-permute-start | bytes 393224 | tf_op jit(solution)/shard_map/ppermute | solution.py:257
  18.9 2.1 %collective-permute-start.14 = (bf16[512,128]{1,0:T(8,128)(2,1)S(1)}, bf16[512,128]{1,0:T(8,128)(2,1)S(1)}, u32[]{:S(2)}, u32[]{:S(2)}) collective-permute-start(bf16[512,128]{1,0:T(8,128)(2,1)S(1)} %get-tuple-element.152), channel_id=1, source_target_pairs={{4,6},{5,7},{12,14},{13,15},{18,20},{19,21},{26,28},{27,29}} | collective-permute-start | bytes 393224 | tf_op jit(solution)/shard_map/ppermute | solution.py:257
  19.6 1.5 %collective-permute-start.16 = (bf16[512,128]{1,0:T(8,128)(2,1)S(1)}, bf16[512,128]{1,0:T(8,128)(2,1)S(1)}, u32[]{:S(2)}, u32[]{:S(2)}) collective-permute-start(bf16[512,128]{1,0:T(8,128)(2,1)S(1)} %get-tuple-element.155), channel_id=1, source_target_pairs={{4,6},{5,7},{12,14},{13,15},{18,20},{19,21},{26,28},{27,29}} | collective-permute-start | bytes 393224 | tf_op jit(solution)/shard_map/ppermute | solution.py:257
  20.4 5.4 %collective-permute-start.18 = (bf16[1024,128]{1,0:T(8,128)(2,1)S(1)}, bf16[1024,128]{1,0:T(8,128)(2,1)S(1)}, u32[]{:S(2)}, u32[]{:S(2)}) collective-permute-start(bf16[1024,128]{1,0:T(8,128)(2,1)S(1)} %get-tuple-element.159), channel_id=1, source_target_pairs={{4,20},{5,21}} | collective-permute-start | bytes 786440 | tf_op jit(solution)/shard_map/ppermute | solution.py:261
  21.1 29.1 %collective-permute-start.21 = (bf16[1024,128]{1,0:T(8,128)(2,1)S(1)}, bf16[1024,128]{1,0:T(8,128)(2,1)S(1)}, u32[]{:S(2)}, u32[]{:S(2)}) collective-permute-start(bf16[1024,128]{1,0:T(8,128)(2,1)S(1)} %get-tuple-element.165), channel_id=1, source_target_pairs={{6,22},{7,23}} | collective-permute-start | bytes 786440 | tf_op jit(solution)/shard_map/ppermute | solution.py:261
  21.8 2.7 %collective-permute-start.17 = (bf16[512,128]{1,0:T(8,128)(2,1)S(1)}, bf16[512,128]{1,0:T(8,128)(2,1)S(1)}, u32[]{:S(2)}, u32[]{:S(2)}) collective-permute-start(bf16[512,128]{1,0:T(8,128)(2,1)S(1)} %get-tuple-element.158), channel_id=1, source_target_pairs={{4,6},{5,7},{12,14},{13,15},{18,20},{19,21},{26,28},{27,29}} | collective-permute-start | bytes 393224 | tf_op jit(solution)/shard_map/ppermute | solution.py:257
  22.5 3.3 %collective-permute-start.19 = (bf16[512,128]{1,0:T(8,128)(2,1)S(1)}, bf16[512,128]{1,0:T(8,128)(2,1)S(1)}, u32[]{:S(2)}, u32[]{:S(2)}) collective-permute-start(bf16[512,128]{1,0:T(8,128)(2,1)S(1)} %get-tuple-element.161), channel_id=1, source_target_pairs={{4,6},{5,7},{12,14},{13,15},{18,20},{19,21},{26,28},{27,29}} | collective-permute-start | bytes 393224 | tf_op jit(solution)/shard_map/ppermute | solution.py:257
  23.2 27.1 %collective-permute-start.20 = (bf16[512,128]{1,0:T(8,128)(2,1)S(1)}, bf16[512,128]{1,0:T(8,128)(2,1)S(1)}, u32[]{:S(2)}, u32[]{:S(2)}) collective-permute-start(bf16[512,128]{1,0:T(8,128)(2,1)S(1)} %get-tuple-element.164), channel_id=1, source_target_pairs={{6,8},{7,9},{20,22},{21,23},{28,30},{29,31}} | collective-permute-start | bytes 393224 | tf_op jit(solution)/shard_map/ppermute | solution.py:257
  24.5 29.8 %collective-permute-start.22 = (bf16[512,128]{1,0:T(8,128)(2,1)S(1)}, bf16[512,128]{1,0:T(8,128)(2,1)S(1)}, u32[]{:S(2)}, u32[]{:S(2)}) collective-permute-start(bf16[512,128]{1,0:T(8,128)(2,1)S(1)} %get-tuple-element.167), channel_id=1, source_target_pairs={{6,8},{7,9},{20,22},{21,23},{28,30},{29,31}} | collective-permute-start | bytes 393224 | tf_op jit(solution)/shard_map/ppermute | solution.py:257
  25.8 35.8 %collective-permute-start.24 = (bf16[1024,128]{1,0:T(8,128)(2,1)S(1)}, bf16[1024,128]{1,0:T(8,128)(2,1)S(1)}, u32[]{:S(2)}, u32[]{:S(2)}) collective-permute-start(bf16[1024,128]{1,0:T(8,128)(2,1)S(1)} %get-tuple-element.171), channel_id=1, source_target_pairs={{6,22},{7,23}} | collective-permute-start | bytes 786440 | tf_op jit(solution)/shard_map/ppermute | solution.py:261
  54.2 10.1 %collective-permute-start.27 = (bf16[1024,128]{1,0:T(8,128)(2,1)S(1)}, bf16[1024,128]{1,0:T(8,128)(2,1)S(1)}, u32[]{:S(2)}, u32[]{:S(2)}) collective-permute-start(bf16[1024,128]{1,0:T(8,128)(2,1)S(1)} %get-tuple-element.177), channel_id=1, source_target_pairs={{8,24},{9,25}} | collective-permute-start | bytes 786440 | tf_op jit(solution)/shard_map/ppermute | solution.py:261
  54.9 6.1 %collective-permute-start.23 = (bf16[512,128]{1,0:T(8,128)(2,1)S(1)}, bf16[512,128]{1,0:T(8,128)(2,1)S(1)}, u32[]{:S(2)}, u32[]{:S(2)}) collective-permute-start(bf16[512,128]{1,0:T(8,128)(2,1)S(1)} %get-tuple-element.170), channel_id=1, source_target_pairs={{6,8},{7,9},{20,22},{21,23},{28,30},{29,31}} | collective-permute-start | bytes 393224 | tf_op jit(solution)/shard_map/ppermute | solution.py:257
  56.2 7.4 %collective-permute-start.25 = (bf16[512,128]{1,0:T(8,128)(2,1)S(1)}, bf16[512,128]{1,0:T(8,128)(2,1)S(1)}, u32[]{:S(2)}, u32[]{:S(2)}) collective-permute-start(bf16[512,128]{1,0:T(8,128)(2,1)S(1)} %get-tuple-element.173), channel_id=1, source_target_pairs={{6,8},{7,9},{20,22},{21,23},{28,30},{29,31}} | collective-permute-start | bytes 393224 | tf_op jit(solution)/shard_map/ppermute | solution.py:257
  57.5 6.8 %collective-permute-start.26 = (bf16[512,128]{1,0:T(8,128)(2,1)S(1)}, bf16[512,128]{1,0:T(8,128)(2,1)S(1)}, u32[]{:S(2)}, u32[]{:S(2)}) collective-permute-start(bf16[512,128]{1,0:T(8,128)(2,1)S(1)} %get-tuple-element.176), channel_id=1, source_target_pairs={{0,2},{1,3},{8,10},{9,11},{22,24},{23,25}} | collective-permute-start | bytes 393224 | tf_op jit(solution)/shard_map/ppermute | solution.py:257
  61.0 3.4 %collective-permute-start.28 = (bf16[512,128]{1,0:T(8,128)(2,1)S(1)}, bf16[512,128]{1,0:T(8,128)(2,1)S(1)}, u32[]{:S(2)}, u32[]{:S(2)}) collective-permute-start(bf16[512,128]{1,0:T(8,128)(2,1)S(1)} %get-tuple-element.179), channel_id=1, source_target_pairs={{0,2},{1,3},{8,10},{9,11},{22,24},{23,25}} | collective-permute-start | bytes 393224 | tf_op jit(solution)/shard_map/ppermute | solution.py:257
  63.6 4.2 %collective-permute-start.30 = (bf16[1024,128]{1,0:T(8,128)(2,1)S(1)}, bf16[1024,128]{1,0:T(8,128)(2,1)S(1)}, u32[]{:S(2)}, u32[]{:S(2)}) collective-permute-start(bf16[1024,128]{1,0:T(8,128)(2,1)S(1)} %get-tuple-element.183), channel_id=1, source_target_pairs={{8,24},{9,25}} | collective-permute-start | bytes 786440 | tf_op jit(solution)/shard_map/ppermute | solution.py:261
  64.4 4.2 %collective-permute-start.33 = (bf16[1024,128]{1,0:T(8,128)(2,1)S(1)}, bf16[1024,128]{1,0:T(8,128)(2,1)S(1)}, u32[]{:S(2)}, u32[]{:S(2)}) collective-permute-start(bf16[1024,128]{1,0:T(8,128)(2,1)S(1)} %get-tuple-element.189), channel_id=1, source_target_pairs={{10,26},{11,27}} | collective-permute-start | bytes 786440 | tf_op jit(solution)/shard_map/ppermute | solution.py:261
  65.1 2.0 %collective-permute-start.29 = (bf16[512,128]{1,0:T(8,128)(2,1)S(1)}, bf16[512,128]{1,0:T(8,128)(2,1)S(1)}, u32[]{:S(2)}, u32[]{:S(2)}) collective-permute-start(bf16[512,128]{1,0:T(8,128)(2,1)S(1)} %get-tuple-element.182), channel_id=1, source_target_pairs={{0,2},{1,3},{8,10},{9,11},{22,24},{23,25}} | collective-permute-start | bytes 393224 | tf_op jit(solution)/shard_map/ppermute | solution.py:257
  65.7 2.1 %collective-permute-start.31 = (bf16[512,128]{1,0:T(8,128)(2,1)S(1)}, bf16[512,128]{1,0:T(8,128)(2,1)S(1)}, u32[]{:S(2)}, u32[]{:S(2)}) collective-permute-start(bf16[512,128]{1,0:T(8,128)(2,1)S(1)} %get-tuple-element.185), channel_id=1, source_target_pairs={{0,2},{1,3},{8,10},{9,11},{22,24},{23,25}} | collective-permute-start | bytes 393224 | tf_op jit(solution)/shard_map/ppermute | solution.py:257
  66.4 2.1 %collective-permute-start.32 = (bf16[512,128]{1,0:T(8,128)(2,1)S(1)}, bf16[512,128]{1,0:T(8,128)(2,1)S(1)}, u32[]{:S(2)}, u32[]{:S(2)}) collective-permute-start(bf16[512,128]{1,0:T(8,128)(2,1)S(1)} %get-tuple-element.188), channel_id=1, source_target_pairs={{2,4},{3,5},{10,12},{11,13},{16,18},{17,19},{24,26},{25,27}} | collective-permute-start | bytes 393224 | tf_op jit(solution)/shard_map/ppermute | solution.py:257
  67.1 1.5 %collective-permute-start.34 = (bf16[512,128]{1,0:T(8,128)(2,1)S(1)}, bf16[512,128]{1,0:T(8,128)(2,1)S(1)}, u32[]{:S(2)}, u32[]{:S(2)}) collective-permute-start(bf16[512,128]{1,0:T(8,128)(2,1)S(1)} %get-tuple-element.191), channel_id=1, source_target_pairs={{2,4},{3,5},{10,12},{11,13},{16,18},{17,19},{24,26},{25,27}} | collective-permute-start | bytes 393224 | tf_op jit(solution)/shard_map/ppermute | solution.py:257
  67.8 4.2 %collective-permute-start.36 = (bf16[1024,128]{1,0:T(8,128)(2,1)S(1)}, bf16[1024,128]{1,0:T(8,128)(2,1)S(1)}, u32[]{:S(2)}, u32[]{:S(2)}) collective-permute-start(bf16[1024,128]{1,0:T(8,128)(2,1)S(1)} %get-tuple-element.195), channel_id=1, source_target_pairs={{10,26},{11,27}} | collective-permute-start | bytes 786440 | tf_op jit(solution)/shard_map/ppermute | solution.py:261
  68.6 4.8 %collective-permute-start.39 = (bf16[1024,128]{1,0:T(8,128)(2,1)S(1)}, bf16[1024,128]{1,0:T(8,128)(2,1)S(1)}, u32[]{:S(2)}, u32[]{:S(2)}) collective-permute-start(bf16[1024,128]{1,0:T(8,128)(2,1)S(1)} %get-tuple-element.201), channel_id=1, source_target_pairs={{12,28},{13,29}} | collective-permute-start | bytes 786440 | tf_op jit(solution)/shard_map/ppermute | solution.py:261
  69.3 2.0 %collective-permute-start.35 = (bf16[512,128]{1,0:T(8,128)(2,1)S(1)}, bf16[512,128]{1,0:T(8,128)(2,1)S(1)}, u32[]{:S(2)}, u32[]{:S(2)}) collective-permute-start(bf16[512,128]{1,0:T(8,128)(2,1)S(1)} %get-tuple-element.194), channel_id=1, source_target_pairs={{2,4},{3,5},{10,12},{11,13},{16,18},{17,19},{24,26},{25,27}} | collective-permute-start | bytes 393224 | tf_op jit(solution)/shard_map/ppermute | solution.py:257
  70.0 2.1 %collective-permute-start.37 = (bf16[512,128]{1,0:T(8,128)(2,1)S(1)}, bf16[512,128]{1,0:T(8,128)(2,1)S(1)}, u32[]{:S(2)}, u32[]{:S(2)}) collective-permute-start(bf16[512,128]{1,0:T(8,128)(2,1)S(1)} %get-tuple-element.197), channel_id=1, source_target_pairs={{2,4},{3,5},{10,12},{11,13},{16,18},{17,19},{24,26},{25,27}} | collective-permute-start | bytes 393224 | tf_op jit(solution)/shard_map/ppermute | solution.py:257
  70.6 2.8 %collective-permute-start.38 = (bf16[512,128]{1,0:T(8,128)(2,1)S(1)}, bf16[512,128]{1,0:T(8,128)(2,1)S(1)}, u32[]{:S(2)}, u32[]{:S(2)}) collective-permute-start(bf16[512,128]{1,0:T(8,128)(2,1)S(1)} %get-tuple-element.200), channel_id=1, source_target_pairs={{4,6},{5,7},{12,14},{13,15},{18,20},{19,21},{26,28},{27,29}} | collective-permute-start | bytes 393224 | tf_op jit(solution)/shard_map/ppermute | solution.py:257
  71.3 2.1 %collective-permute-start.40 = (bf16[512,128]{1,0:T(8,128)(2,1)S(1)}, bf16[512,128]{1,0:T(8,128)(2,1)S(1)}, u32[]{:S(2)}, u32[]{:S(2)}) collective-permute-start(bf16[512,128]{1,0:T(8,128)(2,1)S(1)} %get-tuple-element.203), channel_id=1, source_target_pairs={{4,6},{5,7},{12,14},{13,15},{18,20},{19,21},{26,28},{27,29}} | collective-permute-start | bytes 393224 | tf_op jit(solution)/shard_map/ppermute | solution.py:257
  72.1 6.0 %collective-permute-start.42 = (bf16[1024,128]{1,0:T(8,128)(2,1)S(1)}, bf16[1024,128]{1,0:T(8,128)(2,1)S(1)}, u32[]{:S(2)}, u32[]{:S(2)}) collective-permute-start(bf16[1024,128]{1,0:T(8,128)(2,1)S(1)} %get-tuple-element.207), channel_id=1, source_target_pairs={{12,28},{13,29}} | collective-permute-start | bytes 786440 | tf_op jit(solution)/shard_map/ppermute | solution.py:261
  72.7 4.0 %collective-permute-start.41 = (bf16[512,128]{1,0:T(8,128)(2,1)S(1)}, bf16[512,128]{1,0:T(8,128)(2,1)S(1)}, u32[]{:S(2)}, u32[]{:S(2)}) collective-permute-start(bf16[512,128]{1,0:T(8,128)(2,1)S(1)} %get-tuple-element.206), channel_id=1, source_target_pairs={{4,6},{5,7},{12,14},{13,15},{18,20},{19,21},{26,28},{27,29}} | collective-permute-start | bytes 393224 | tf_op jit(solution)/shard_map/ppermute | solution.py:257
  73.5 30.9 %collective-permute-start.44 = (bf16[1024,128]{1,0:T(8,128)(2,1)S(1)}, bf16[1024,128]{1,0:T(8,128)(2,1)S(1)}, u32[]{:S(2)}, u32[]{:S(2)}) collective-permute-start(bf16[1024,128]{1,0:T(8,128)(2,1)S(1)} %get-tuple-element.212), channel_id=1, source_target_pairs={{14,30},{15,31}} | collective-permute-start | bytes 786440 | tf_op jit(solution)/shard_map/ppermute | solution.py:261
  74.8 3.3 %collective-permute-start.43 = (bf16[512,128]{1,0:T(8,128)(2,1)S(1)}, bf16[512,128]{1,0:T(8,128)(2,1)S(1)}, u32[]{:S(2)}, u32[]{:S(2)}) collective-permute-start(bf16[512,128]{1,0:T(8,128)(2,1)S(1)} %get-tuple-element.209), channel_id=1, source_target_pairs={{4,6},{5,7},{12,14},{13,15},{18,20},{19,21},{26,28},{27,29}} | collective-permute-start | bytes 393224 | tf_op jit(solution)/shard_map/ppermute | solution.py:257
  75.5 23.8 %collective-permute-start.46 = (bf16[512,128]{1,0:T(8,128)(2,1)S(1)}, bf16[512,128]{1,0:T(8,128)(2,1)S(1)}, u32[]{:S(2)}, u32[]{:S(2)}) collective-permute-start(bf16[512,128]{1,0:T(8,128)(2,1)S(1)} %get-tuple-element.214), channel_id=1, source_target_pairs={{6,8},{7,9},{20,22},{21,23},{28,30},{29,31}} | collective-permute-start | bytes 393224 | tf_op jit(solution)/shard_map/ppermute | solution.py:257
  76.8 26.2 %collective-permute-start.45 = (bf16[512,128]{1,0:T(8,128)(2,1)S(1)}, bf16[512,128]{1,0:T(8,128)(2,1)S(1)}, u32[]{:S(2)}, u32[]{:S(2)}) collective-permute-start(bf16[512,128]{1,0:T(8,128)(2,1)S(1)} %get-tuple-element.213), channel_id=1, source_target_pairs={{6,8},{7,9},{20,22},{21,23},{28,30},{29,31}} | collective-permute-start | bytes 393224 | tf_op jit(solution)/shard_map/ppermute | solution.py:257
  104.7 21.6 %collective-permute-start.47 = (bf16[768,256]{1,0:T(8,128)(2,1)S(1)}, bf16[768,256]{1,0:T(8,128)(2,1)S(1)}, u32[]{:S(2)}, u32[]{:S(2)}) collective-permute-start(bf16[768,256]{1,0:T(8,128)(2,1)S(1)} %get-tuple-element.215), channel_id=1, source_target_pairs={{0,1},{1,0},{2,3},{3,2},{4,5},{5,4},{6,7},{7,6},{8,9},{9,8},{10,11... | collective-permute-start | bytes 1179656 | tf_op jit(solution)/shard_map/ppermute | solution.py:274
  119.9 11.2 %collective-permute-start.48 = (bf16[1024,128]{1,0:T(8,128)(2,1)S(1)}, bf16[1024,128]{1,0:T(8,128)(2,1)S(1)}, u32[]{:S(2)}, u32[]{:S(2)}) collective-permute-start(bf16[1024,128]{1,0:T(8,128)(2,1)S(1)} %get-tuple-element.219), channel_id=1, source_target_pairs={{14,30},{15,31}} | collective-permute-start | bytes 786440 | tf_op jit(solution)/shard_map/ppermute | solution.py:261
  121.2 7.0 %collective-permute-start.50 = (bf16[512,128]{1,0:T(8,128)(2,1)S(1)}, bf16[512,128]{1,0:T(8,128)(2,1)S(1)}, u32[]{:S(2)}, u32[]{:S(2)}) collective-permute-start(bf16[512,128]{1,0:T(8,128)(2,1)S(1)} %get-tuple-element.221), channel_id=1, source_target_pairs={{6,8},{7,9},{20,22},{21,23},{28,30},{29,31}} | collective-permute-start | bytes 393224 | tf_op jit(solution)/shard_map/ppermute | solution.py:257
  122.5 8.4 %collective-permute-start.49 = (bf16[512,128]{1,0:T(8,128)(2,1)S(1)}, bf16[512,128]{1,0:T(8,128)(2,1)S(1)}, u32[]{:S(2)}, u32[]{:S(2)}) collective-permute-start(bf16[512,128]{1,0:T(8,128)(2,1)S(1)} %get-tuple-element.220), channel_id=1, source_target_pairs={{6,8},{7,9},{20,22},{21,23},{28,30},{29,31}} | collective-permute-start | bytes 393224 | tf_op jit(solution)/shard_map/ppermute | solution.py:257
  131.4 3.3 %collective-permute-start.51 = (bf16[768,256]{1,0:T(8,128)(2,1)S(1)}, bf16[768,256]{1,0:T(8,128)(2,1)S(1)}, u32[]{:S(2)}, u32[]{:S(2)}) collective-permute-start(bf16[768,256]{1,0:T(8,128)(2,1)S(1)} %get-tuple-element.222), channel_id=1, source_target_pairs={{0,1},{1,0},{2,3},{3,2},{4,5},{5,4},{6,7},{7,6},{8,9},{9,8},{10,11... | collective-permute-start | bytes 1179656 | tf_op jit(solution)/shard_map/ppermute | solution.py:274
